TPU v7x, 256 devices: a whole 4x4x8 slice. The times are simulated.
256 devices in a mesh: ctx: 128 (over z, x, y), pb: 2 (over core).
Axes of the slice: x: 4, y: 4, z: 8, core: 2. Of those that a mesh axis runs over, the one named last changes fastest.
Arguments:
- queries: bfloat16 [64, 512, 2048], P('pb', 'ctx'), may hold values from -100 to 100
- key_blocks: bfloat16 [512, 512, 512], P('ctx'), may hold values from -12 to 12
- value_blocks: bfloat16 [512, 512, 512], P('ctx'), may hold values from -6 to 6
- selected: int32 [64, 3], replicated, may hold values from 0 to 447, as said below
Outputs:
- attended: bfloat16 [64, 512, 2048], P('pb', 'ctx')
Inputs may be any that keep to these rules, and one draw needn't show every extreme that they name: `selected`: row b names 3 different KV blocks, all before block 448. Query blocks b < 32 form pb group 0, the others group 1. Counting own blocks too, the KV blocks kept by one ctx index are named by query blocks of one pb group only, and at most 4 times in all; some ctx index is named exactly 4 times.
All inputs are finite; a program needn't handle non-finite values.
Results may differ from a plain program's by a relative error of at most 0.0051.
Values may be sent and summed in bfloat16 or wider, within the bound.
No kernel may reach another device: no remote copies, remote signals or barrier semaphores. Data moves between devices by JAX's collectives and lax.ppermute only.
A program may use at most 192 MiB of HBM per device.

v0:
```python
import math

import jax
import jax.numpy as jnp
from jax import lax
from jax.sharding import PartitionSpec as P

HD = 128
TOPK = 3
MOST = 4


def in_blocks(value, dim, count):
    dims = value.shape
    pieces = value.reshape(*dims[:dim], count, dims[dim] // count, *dims[dim + 1 :])
    return jnp.moveaxis(pieces, dim, 0)


def laid_out(pieces, dim):
    dims = list(pieces.shape[1:])
    dims[dim] *= pieces.shape[0]
    return jnp.moveaxis(pieces, 0, dim).reshape(dims)


def one_exchange(value, axis, axes, splits, concats):
    sizes = [lax.axis_size(a) for a in axes]
    pieces = in_blocks(value, splits[0], sizes[0])
    pieces = jnp.moveaxis(in_blocks(pieces, splits[1] + 1, sizes[1]), 0, 1)
    inside = pieces.shape[2:]
    pieces = pieces.reshape(-1, *inside)
    pieces = lax.all_to_all(pieces, axis, split_axis=0, concat_axis=0, tiled=True)
    pieces = laid_out(pieces.reshape(*sizes, *inside), concats[0] + 1)
    return laid_out(pieces, concats[1])


def routing_tables(selected, kv_count, ctx_size):
    block_total = selected.shape[0]
    kv_total = kv_count * ctx_size
    own_block = kv_total - block_total + jnp.arange(block_total, dtype=jnp.int32)
    targets = jnp.concatenate([own_block[:, None], selected], axis=1)
    flat_targets = targets.reshape(-1)
    owner_of = flat_targets // kv_count
    matches = (owner_of[:, None] == jnp.arange(ctx_size, dtype=jnp.int32)[None, :]).astype(
        jnp.int32
    )
    earlier = jnp.cumsum(matches, axis=0) - matches
    slot_rank = jnp.sum(earlier * matches, axis=1)
    return (flat_targets, owner_of, slot_rank)


def slot_table(owner_of, slot_rank, ctx_size):
    slot_ids = slot_rank * ctx_size + owner_of
    pair_ids = jnp.arange(owner_of.shape[0], dtype=jnp.int32)
    matches = slot_ids[:, None] == jnp.arange(MOST * ctx_size, dtype=jnp.int32)[None, :]
    return jnp.sum(jnp.where(matches, pair_ids[:, None] + 1, 0), axis=0) - 1


def partial_block(q_rows, k_blk, v_blk, positions, is_causal):
    row_count = q_rows.shape[0]
    groups = k_blk.shape[1] // HD
    per_group = q_rows.shape[1] // k_blk.shape[1]
    q_heads = q_rows.reshape(row_count, groups, per_group, HD)
    k_heads = k_blk.reshape(k_blk.shape[0], groups, HD)
    v_heads = v_blk.reshape(v_blk.shape[0], groups, HD)
    scores = jnp.einsum("rghd,kgd->ghrk", q_heads, k_heads, preferred_element_type=jnp.float32) * (
        1.0 / math.sqrt(HD)
    )
    key_pos = jnp.arange(k_blk.shape[0], dtype=jnp.int32)
    allowed = jnp.logical_or(key_pos[None, :] <= positions[:, None], jnp.logical_not(is_causal))
    scores = jnp.where(allowed, scores, -jnp.inf)
    block_max = jnp.max(scores, axis=-1)
    weights = jnp.exp(scores - block_max[..., None]).astype(jnp.bfloat16)
    block_sum = jnp.sum(weights, axis=-1, dtype=jnp.float32)
    partial_value = jnp.einsum(
        "ghrk,kgd->rghd", weights, v_heads, preferred_element_type=jnp.float32
    )
    partial_value = partial_value / jnp.transpose(block_sum, (2, 0, 1))[..., None]
    return (
        partial_value.astype(jnp.bfloat16).reshape(row_count, -1),
        jnp.transpose(block_max, (2, 0, 1)).reshape(row_count, -1),
        jnp.transpose(block_sum, (2, 0, 1)).reshape(row_count, -1),
    )


def attend_slots(gathered, key_blocks, value_blocks, local_kv, causal_flags, positions):

    def single(slot_item):
        q_rows, kv_index, is_causal = slot_item
        k_blk = lax.dynamic_index_in_dim(key_blocks, kv_index, 0, keepdims=False)
        v_blk = lax.dynamic_index_in_dim(value_blocks, kv_index, 0, keepdims=False)
        return partial_block(q_rows, k_blk, v_blk, positions, is_causal)

    return lax.map(single, (gathered, local_kv, causal_flags))


def combine_parts(part_out, maxima, totals, head_count):
    best_max = jnp.max(maxima, axis=1, keepdims=True)
    scales = jnp.exp(maxima - best_max) * totals
    shaped = part_out.reshape(part_out.shape[:3] + (head_count, HD))
    summed = jnp.sum(shaped.astype(jnp.float32) * scales[..., None], axis=1)
    result = summed / jnp.sum(scales, axis=1)[..., None]
    return result.reshape(part_out.shape[0], part_out.shape[2], part_out.shape[3]).astype(
        jnp.bfloat16
    )


def local(queries, key_blocks, value_blocks, selected):
    ctx_size = lax.axis_size("ctx")
    core_count = lax.axis_size("pb")
    ctx_place = lax.axis_index("ctx")
    group_idx = lax.axis_index("pb")
    half_blocks, row_count, feat_width = queries.shape
    kv_count = key_blocks.shape[0]
    head_count = feat_width // HD
    stride = TOPK + 1
    flat_targets, owner_of, slot_rank = routing_tables(selected, kv_count, ctx_size)
    slot_pairs = slot_table(owner_of, slot_rank, ctx_size)
    local_query = slot_pairs // stride - group_idx * half_blocks
    is_valid = (slot_pairs >= 0) & (local_query >= 0) & (local_query < half_blocks)
    my_slots = lax.dynamic_slice_in_dim(slot_pairs.reshape(MOST, ctx_size), ctx_place, 1, 1)[:, 0]
    my_pairs_safe = jnp.maximum(my_slots, 0)
    local_kv = jnp.clip(
        jnp.take(flat_targets, my_pairs_safe) - ctx_place * kv_count, 0, kv_count - 1
    )
    causal_flags = (my_slots >= 0) & (my_slots % stride == 0)
    slot_groups = my_pairs_safe // stride // half_blocks
    my_pairs = group_idx * half_blocks * stride + jnp.arange(half_blocks * stride, dtype=jnp.int32)
    fetch_index = jnp.take(slot_rank, my_pairs) * ctx_size + jnp.take(owner_of, my_pairs)
    half_rows = row_count // core_count
    picked = jnp.take(queries, jnp.clip(local_query, 0, half_blocks - 1), axis=0)
    picked = jnp.where(is_valid[:, None, None], picked, jnp.zeros_like(picked))
    outgoing = picked.reshape(MOST, ctx_size, core_count, half_rows, feat_width)
    arrived = one_exchange(outgoing, ("ctx", "pb"), ("ctx", "pb"), (1, 2), (1, 2))
    chosen = arrived[:, :, 0]
    chosen = jnp.where((slot_groups == 1)[:, None, None, None], arrived[:, :, 1], chosen)
    positions = (
        jnp.arange(ctx_size, dtype=jnp.int32)[:, None] * row_count
        + group_idx * half_rows
        + jnp.arange(half_rows, dtype=jnp.int32)[None, :]
    ).reshape(-1)
    part_out, maxima, totals = attend_slots(
        chosen.reshape(MOST, ctx_size * half_rows, feat_width),
        key_blocks,
        value_blocks,
        local_kv,
        causal_flags,
        positions,
    )
    spread_parts = jnp.broadcast_to(
        part_out.reshape(MOST, ctx_size, 1, half_rows, feat_width),
        (MOST, ctx_size, core_count, half_rows, feat_width),
    )
    returned = one_exchange(spread_parts, ("ctx", "pb"), ("ctx", "pb"), (1, 2), (1, 2))
    spread_max = jnp.broadcast_to(
        maxima.reshape(MOST, ctx_size, 1, half_rows * head_count),
        (MOST, ctx_size, core_count, half_rows * head_count),
    )
    spread_sum = jnp.broadcast_to(
        totals.reshape(MOST, ctx_size, 1, half_rows * head_count),
        (MOST, ctx_size, core_count, half_rows * head_count),
    )
    got_max, got_sum = (
        one_exchange(spread_max, ("ctx", "pb"), ("ctx", "pb"), (1, 2), (1, 2)),
        one_exchange(spread_sum, ("ctx", "pb"), ("ctx", "pb"), (1, 2), (1, 2)),
    )
    flat_parts = returned.reshape(MOST * ctx_size, row_count, feat_width)
    my_parts = jnp.take(flat_parts, fetch_index, axis=0).reshape(
        half_blocks, stride, row_count, feat_width
    )
    my_max = jnp.take(got_max.reshape(MOST * ctx_size, row_count, head_count), fetch_index, axis=0)
    my_sum = jnp.take(got_sum.reshape(MOST * ctx_size, row_count, head_count), fetch_index, axis=0)
    my_max = my_max.reshape(half_blocks, stride, row_count, head_count)
    my_sum = my_sum.reshape(half_blocks, stride, row_count, head_count)
    return combine_parts(my_parts, my_max, my_sum, head_count)


def solution(mesh):
    in_specs = (P("pb", "ctx", None), P("ctx", None, None), P("ctx", None, None), P())
    out_specs = P("pb", "ctx", None)
    return jax.shard_map(local, mesh=mesh, in_specs=in_specs, out_specs=out_specs, check_vma=False)
```

profile of v0, /device:TPU:2, one launch (start us, length us, event | category | flops | bytes accessed | tf_op | source)
XLA Modules:
  0.0 653.8 jit_solution(13789333185172448165)
XLA Ops:
  2.0 16.7 %gather_fusion.1 = bf16[512,4,2048]{2,1,0:T(4,128)(2,1)} fusion(bf16[32,4,2048]{2,1,0:T(4,128)(2,1)S(1)} %copy-done, s32[1024]{0:T(1024)S(1)} %pad_clamp_fusion.1), kind=kCustom, calls=%fused_computation.5 | custom fusion | bytes 16779264 | tf_op jit(solution)/shard_map/jit(_take)/gather | solution.py:130
  18.7 17.7 %gather.24 = bf16[4,128,1,2,2,2048]{5,4,3,1,0,2:T(2,128)(2,1)} reshape(bf16[512,4,2048]{2,1,0:T(4,128)(2,1)} %gather_fusion.1) | data formatting | bytes 16777216 | tf_op jit(solution)/shard_map/jit(_take)/gather | solution.py:130
  36.6 14.2 %broadcast_select_fusion.1 = bf16[4,128,1,2,2,2048]{5,4,0,3,1,2:T(2,128)(2,1)} fusion(pred[4,128]{0,1:T(8,128)(4,1)S(1)} %copy.150, pred[4,128]{0,1:T(8,128)(4,1)S(1)} %copy.151, bf16[4,128,1,2,2,2048]{5,4,3,1,0,2:T(2,128)(2,1)} %gather.24), kind=kLoop, calls=%fused_computation.27 | loop fusion | flops 8388608 | bytes 16778240 | tf_op jit(solution)/shard_map/jit(_where)/select_n | solution.py:131
  50.8 15.7 %all-to-all-start = ((bf16[256,4,1,1,2,2048]{5,4,1,3,2,0:T(2,128)(2,1)}), bf16[256,4,1,1,2,2048]{5,4,1,3,2,0:T(2,128)(2,1)}, u32[]{:S(2)}, u32[]{:S(2)}) async-start(bf16[256,4,1,1,2,2048]{5,4,1,3,2,0:T(2,128)(2,1)} %bitcast.169), calls=%async_computation | async-start | bytes 16777216 | tf_op jit(solution)/shard_map/all_to_all | solution.py:31
  67.6 185.3 %all-to-all-done = bf16[256,4,1,1,2,2048]{5,4,1,3,2,0:T(2,128)(2,1)} async-done(((bf16[256,4,1,1,2,2048]{5,4,1,3,2,0:T(2,128)(2,1)}), bf16[256,4,1,1,2,2048]{5,4,1,3,2,0:T(2,128)(2,1)}, u32[]{:S(2)}, u32[]{:S(2)}) %all-to-all-start) | async-done | bytes 8388640 | tf_op jit(solution)/shard_map/all_to_all | solution.py:31
  252.9 7.8 %fusion.22 = (bf16[4,128,1,2,2048]{4,3,0,2,1:T(2,128)(2,1)S(1)}, bf16[4,128,1,2,2048]{4,3,0,2,1:T(2,128)(2,1)S(1)}) fusion(bf16[4,128,2,2,2048]{4,3,0,2,1:T(2,128)(2,1)} %bitcast.14), kind=kLoop, calls=%fused_computation.104 | loop fusion | bytes 16777216 | tf_op jit(solution)/shard_map/slice | solution.py:135
  269.2 4.7 bitcast_select_fusion.1
  273.9 7.7 %copy.157 = bf16[4,256,2048]{1,2,0:T(8,128)(2,1)} copy(bf16[4,256,2048]{2,0,1:T(4,128)(2,1)} %bitcast_select_fusion.1) | data formatting | bytes 8388608
  281.6 76.9 %while.15 = (s32[]{:T(128)}, bf16[4,256,2048]{1,2,0:T(8,128)(2,1)}, f32[4,256,16]{1,2,0:T(8,128)S(1)}, f32[4,256,16]{1,2,0:T(8,128)S(1)}, s32[4]{0:T(128)S(1)}, ...) while((s32[]{:T(128)}, bf16[4,256,2048]{1,2,0:T(8,128)(2,1)}, ...), condition=%wide.region_7.9_spmd.clone, body=%wide.region_4.8_spmd.clone.sunk | while | flops 1102307584 | bytes 70997216 | solution.py:93
  294.1 5.6 fusion.39
  313.4 5.6 fusion.39
  332.6 5.6 fusion.39
  351.8 5.6 fusion.39
  360.1 7.0 %all-to-all-start.3 = ((f32[256,1,128]{2,1,0:T(1,128)}), f32[256,1,128]{2,1,0:T(1,128)S(1)}, u32[]{:S(2)}, u32[]{:S(2)}) async-start(f32[256,1,128]{2,1,0:T(1,128)} %reshape.475), calls=%async_computation.3 | async-start | bytes 262144 | tf_op jit(solution)/shard_map/all_to_all | solution.py:31
  368.7 10.4 %all-to-all-done.3 = f32[256,1,128]{2,1,0:T(1,128)S(1)} async-done(((f32[256,1,128]{2,1,0:T(1,128)}), f32[256,1,128]{2,1,0:T(1,128)S(1)}, u32[]{:S(2)}, u32[]{:S(2)}) %all-to-all-start.3) | async-done | bytes 131104 | tf_op jit(solution)/shard_map/all_to_all | solution.py:31
  379.1 6.8 %all-to-all-start.2 = ((f32[256,1,128]{2,1,0:T(1,128)}), f32[256,1,128]{2,1,0:T(1,128)S(1)}, u32[]{:S(2)}, u32[]{:S(2)}) async-start(f32[256,1,128]{2,1,0:T(1,128)} %reshape.477), calls=%async_computation.2 | async-start | bytes 262144 | tf_op jit(solution)/shard_map/all_to_all | solution.py:31
  385.9 8.0 %copy.158 = bf16[4,256,2048]{2,0,1:T(4,128)(2,1)} copy(bf16[4,256,2048]{1,2,0:T(8,128)(2,1)} %get-tuple-element.61) | data formatting | bytes 8388608 | tf_op jit(solution)/shard_map/while | solution.py:93
  393.9 12.6 %copy.159 = bf16[4,128,2,2048]{3,2,0,1:T(2,128)(2,1)} copy(bf16[4,128,2,2048]{3,0,2,1:T(4,128)(2,1)} %bitcast.172) | data formatting | bytes 8388608 | tf_op jit(solution)/shard_map/broadcast_in_dim | solution.py:149
  406.5 8.6 %reshape.379 = bf16[4,128,1,2,2,2048]{5,4,0,3,1,2:T(2,128)(2,1)} broadcast(bf16[4,128,2,2048]{3,2,0,1:T(2,128)(2,1)} %copy.159), dimensions={0,1,4,5} | broadcast | bytes 12582912 | tf_op jit(solution)/shard_map/reshape | solution.py:15
  415.1 15.3 %all-to-all-start.1 = ((bf16[256,4,1,1,2,2048]{5,4,1,3,2,0:T(2,128)(2,1)}), bf16[256,4,1,1,2,2048]{5,4,1,3,2,0:T(2,128)(2,1)}, u32[]{:S(2)}, u32[]{:S(2)}) async-start(bf16[256,4,1,1,2,2048]{5,4,1,3,2,0:T(2,128)(2,1)} %bitcast.168), calls=%async_computation.1 | async-start | bytes 16777216 | tf_op jit(solution)/shard_map/all_to_all | solution.py:31
  440.2 176.4 %all-to-all-done.1 = bf16[256,4,1,1,2,2048]{5,4,1,3,2,0:T(2,128)(2,1)} async-done(((bf16[256,4,1,1,2,2048]{5,4,1,3,2,0:T(2,128)(2,1)}), bf16[256,4,1,1,2,2048]{5,4,1,3,2,0:T(2,128)(2,1)}, u32[]{:S(2)}, u32[]{:S(2)}) %all-to-all-start.1) | async-done | bytes 8388640 | tf_op jit(solution)/shard_map/all_to_all | solution.py:31
  616.6 11.2 %copy.160 = bf16[4,128,2,1,2,2048]{5,1,0,4,2,3:T(8,128)(2,1)} copy(bf16[4,128,2,1,2,2048]{5,4,0,2,1,3:T(2,128)(2,1)} %bitcast.29) | data formatting | bytes 16777216 | tf_op jit(solution)/shard_map/transpose | solution.py:22
  627.8 12.4 %copy.161 = bf16[512,4,2048]{2,1,0:T(4,128)(2,1)} copy(bf16[512,4,2048]{2,0,1:T(8,128)(2,1)} %bitcast.170) | data formatting | bytes 16777216 | tf_op jit(solution)/shard_map/reshape;reshape | solution.py:166
  640.3 7.0 %gather_fusion.2 = bf16[128,4,2048]{2,1,0:T(4,128)(2,1)} fusion(bf16[512,4,2048]{2,1,0:T(4,128)(2,1)} %copy.161, s32[1024]{0:T(1024)S(1)} %pad_clamp_fusion), kind=kCustom, calls=%fused_computation.6 | custom fusion | bytes 4194816 | tf_op jit(solution)/shard_map/jit(_take)/gather | solution.py:167
  (151 shorter events, 75.1 us)
Async XLA Ops:
  0.0 2.0 copy-start
  50.8 202.1 %all-to-all-start = ((bf16[256,4,1,1,2,2048]{5,4,1,3,2,0:T(2,128)(2,1)}), bf16[256,4,1,1,2,2048]{5,4,1,3,2,0:T(2,128)(2,1)}, u32[]{:S(2)}, u32[]{:S(2)}) async-start(bf16[256,4,1,1,2,2048]{5,4,1,3,2,0:T(2,128)(2,1)} %bitcast.169), calls=%async_computation | async-start | bytes 16777216 | tf_op jit(solution)/shard_map/all_to_all | solution.py:31
  289.6 3.2 copy-start.2
  308.8 3.2 copy-start.2
  328.1 3.2 copy-start.2
  347.3 3.2 copy-start.2
  360.1 19.0 %all-to-all-start.3 = ((f32[256,1,128]{2,1,0:T(1,128)}), f32[256,1,128]{2,1,0:T(1,128)S(1)}, u32[]{:S(2)}, u32[]{:S(2)}) async-start(f32[256,1,128]{2,1,0:T(1,128)} %reshape.475), calls=%async_computation.3 | async-start | bytes 262144 | tf_op jit(solution)/shard_map/all_to_all | solution.py:31
  379.1 27.4 %all-to-all-start.2 = ((f32[256,1,128]{2,1,0:T(1,128)}), f32[256,1,128]{2,1,0:T(1,128)S(1)}, u32[]{:S(2)}, u32[]{:S(2)}) async-start(f32[256,1,128]{2,1,0:T(1,128)} %reshape.477), calls=%async_computation.2 | async-start | bytes 262144 | tf_op jit(solution)/shard_map/all_to_all | solution.py:31
  415.1 201.5 %all-to-all-start.1 = ((bf16[256,4,1,1,2,2048]{5,4,1,3,2,0:T(2,128)(2,1)}), bf16[256,4,1,1,2,2048]{5,4,1,3,2,0:T(2,128)(2,1)}, u32[]{:S(2)}, u32[]{:S(2)}) async-start(bf16[256,4,1,1,2,2048]{5,4,1,3,2,0:T(2,128)(2,1)} %bitcast.168), calls=%async_computation.1 | async-start | bytes 16777216 | tf_op jit(solution)/shard_map/all_to_all | solution.py:31
  640.3 13.1 %copy-start.1 = (bf16[32,4,2048]{2,1,0:T(4,128)(2,1)S(1)}, bf16[32,4,2048]{2,1,0:T(4,128)(2,1)}, u32[]{:S(2)}) copy-start(bf16[32,4,2048]{2,1,0:T(4,128)(2,1)} %param.10) | copy-start | bytes 1572868
where the time goes:
time: 662 us; the launch traced here: 654 us
  waiting for transfers between devices  372 us (56%)
  local copies, waits for them, and re-layouts  165 us (25%)
  starting transfers between devices  44.8 us (7%)
  other arithmetic  33 us (5%)
  matrix products  27.9 us (4%)
  loops' own time  9.99 us (2%)
    all_to_all x4, waiting for transfers between devices, one_exchange(): lax.all_to_all(pieces, axis, split_axis=0, concat_axis=0, tiled=True)  372 us
    all_to_all x4, starting transfers between devices, one_exchange(): lax.all_to_all(pieces, axis, split_axis=0, concat_axis=0, tiled=True)  44.8 us
    gather x2, local copies, waits for them, and re-layouts, local(): jnp.take(queries, jnp.clip(local_query, 0, half_blocks - 1), axis=0)  34.4 us
    dot_general x4, matrix products, partial_block(): jnp.einsum('ghrk,kgd->rghd', weights, v_heads, preferred_element_type=jnp...  22.3 us
    select_n x1, other arithmetic, local(): picked = jnp.where(is_valid[:, None, None], picked, jnp.zeros_like(picked))  14.2 us
  transfers between devices with their start and end apart: 4, of which 3 were waited for; matrix products, arithmetic and copies ran while one was open for 5% of the time, Pallas kernels for 0%

commit v1 on v0

v1 whole, which is shorter than its diff:
```python
import functools
import math

import jax
import jax.numpy as jnp
from jax import lax
from jax.experimental import pallas as pl
from jax.experimental.pallas import tpu as pltpu
from jax.sharding import Mesh, PartitionSpec as P

HD = 128
CTX = ("zp", "zl", "x", "y")
PAIR = ("zl", "x", "y", "c")


def exchange(value, axes):
    return lax.all_to_all(value, axes, split_axis=0, concat_axis=0, tiled=True)


def pick_kernel(index_ref, table_ref, out_ref):
    def body(step, carry):
        for inner in range(8):
            place = step * 8 + inner
            out_ref[place] = table_ref[index_ref[place]]
        return carry

    lax.fori_loop(0, out_ref.shape[0] // 8, body, 0)


def pick(index, table):
    count = index.shape[0]
    return pl.pallas_call(
        pick_kernel,
        out_shape=jax.ShapeDtypeStruct((count,) + table.shape[1:], table.dtype),
        in_specs=[
            pl.BlockSpec(memory_space=pltpu.SMEM),
            pl.BlockSpec(memory_space=pltpu.VMEM),
        ],
        out_specs=pl.BlockSpec(memory_space=pltpu.VMEM),
        name="pick",
    )(index, table)


def attend_kernel(own_keys, heads, q_ref, k_ref, v_ref, out_ref):
    rows = q_ref.shape[0]
    nt = (((1,), (1,)), ((), ()))
    scores = lax.dot_general(q_ref[...], k_ref[...], nt, preferred_element_type=jnp.float32)
    first = pl.program_id(0) * (rows // heads)
    token = first + lax.broadcasted_iota(jnp.int32, (rows, own_keys), 0) // heads
    key = lax.broadcasted_iota(jnp.int32, (rows, own_keys), 1)
    own = jnp.where(key_place(key, own_keys) <= token, scores[:, :own_keys], -jnp.inf)
    scores = jnp.concatenate([own, scores[:, own_keys:]], axis=1)
    best = jnp.max(scores, axis=1, keepdims=True)
    weights = jnp.exp((scores - best) * (1.0 / math.sqrt(HD))).astype(jnp.bfloat16)
    total = jnp.sum(weights.astype(jnp.float32), axis=1, keepdims=True)
    mixed = jnp.dot(weights, v_ref[...], preferred_element_type=jnp.float32)
    out_ref[...] = (mixed / total).astype(out_ref.dtype)


def key_place(key, own_keys):
    piece, inner = key // 8, key % 8
    return (piece % 2) * (own_keys // 2) + (piece // 2) * 8 + inner


def attend(q_rows, keys, values, own_keys, heads):
    rows, tile = q_rows.shape[0], 256
    whole = pl.BlockSpec(keys.shape, lambda i: (0, 0))
    part = pl.BlockSpec((tile, HD), lambda i: (i, 0))
    return pl.pallas_call(
        functools.partial(attend_kernel, own_keys, heads),
        grid=(rows // tile,),
        out_shape=jax.ShapeDtypeStruct(q_rows.shape, jnp.bfloat16),
        in_specs=[part, whole, whole],
        out_specs=part,
        name="attend",
    )(q_rows, keys, values)


def local(queries, key_blocks, value_blocks, selected):
    core = lax.axis_index("c")
    half_blocks, row_count, feat_width = queries.shape
    kv_count, block, kv_width = key_blocks.shape
    groups = kv_width // HD
    heads = feat_width // kv_width
    ctx_size = lax.axis_size(CTX)
    pair_size = lax.axis_size(PAIR)
    spots = ctx_size // groups
    piece = block // pair_size
    block_total = selected.shape[0]

    def spread(blocks):
        mine = lax.dynamic_slice_in_dim(blocks, core * (block // 2), block // 2, 1)
        mine = mine.reshape(kv_count, spots, piece, groups, HD)
        mine = mine.transpose(3, 1, 0, 2, 4).reshape(ctx_size, kv_count * piece, HD)
        return exchange(mine, CTX).reshape(ctx_size * kv_count, piece, HD)

    own_block = ctx_size * kv_count - block_total + jnp.arange(block_total, dtype=jnp.int32)
    targets = jnp.concatenate([own_block[:, None], selected], axis=1)
    width = targets.shape[1]
    index = targets.reshape(2, half_blocks, width).transpose(1, 0, 2).reshape(-1)

    def deliver(pieces):
        sent = pick(index, pieces).reshape(pair_size, width * piece, HD)
        got = exchange(sent, PAIR).reshape(pair_size, width, piece, HD)
        return got.transpose(1, 0, 2, 3).reshape(width * block, HD)

    keys = deliver(spread(key_blocks))
    values = deliver(spread(value_blocks))
    asked = queries.reshape(half_blocks, row_count, groups, heads, HD)
    asked = asked.transpose(2, 0, 1, 3, 4).reshape(ctx_size, row_count * heads, HD)
    asked = exchange(asked, CTX).reshape(-1, HD)
    done = attend(asked, keys, values, block, heads)
    back = exchange(done.reshape(ctx_size, row_count * heads, HD), CTX)
    back = back.reshape(groups, half_blocks, row_count, heads, HD)
    return back.transpose(1, 2, 0, 3, 4).reshape(queries.shape)


def solution(mesh):
    z_pairs = 4
    ctx_size, cores = mesh.devices.shape
    plane = 4
    fine = mesh.devices.reshape(z_pairs, ctx_size // (z_pairs * plane * plane), plane, plane, cores)
    fine_mesh = Mesh(fine, ("zp", "zl", "x", "y", "c"))
    in_specs = (P("c", CTX, None), P(CTX, None, None), P(CTX, None, None), P())
    out_specs = P("c", CTX, None)
    return jax.shard_map(
        local, mesh=fine_mesh, in_specs=in_specs, out_specs=out_specs, check_vma=False
    )
```

time: 662 us -> 187 us (0.28); the launches traced: 654 us -> 186 us
  waiting for transfers between devices: 372 us -> 93.2 us
  local copies, waits for them, and re-layouts: 165 us -> 10.3 us
  other arithmetic: 33 us -> 0.02 us
  matrix products: 27.9 us -> 0 us
  blocking collectives: 0 us -> 25.5 us
  Pallas kernels: 0 us -> 16.6 us
  loops' own time: 9.99 us -> 0 us
    all_to_all x4 -> x5, waiting for transfers between devices: 372 us -> 93.2 us  [exchange(): return lax.all_to_all(value, axes, split_axis=0, concat_axis=0, tiled=True)]
    gather x9 -> x0, local copies, waits for them, and re-layouts: 49.2 us -> none  [the longest x2 34.4 us: local(): jnp.take(queries, jnp.clip(local_query, 0, half_blocks - 1), axis=0)]
    dot_general x8 -> x0, matrix products: 27.9 us -> none  [the longest x4 22.3 us: partial_block(): jnp.einsum('ghrk,kgd->rghd', weights, v_heads, preferred_element_type=jnp...]
    all_to_all x0 -> x1, blocking collectives: none -> 25.5 us  [exchange(): return lax.all_to_all(value, axes, split_axis=0, concat_axis=0, tiled=True)]
    dynamic_slice x28 -> x0, local copies, waits for them, and re-layouts: 20.5 us -> none  [the longest x12 10.1 us: attend_slots(): return lax.map(single, (gathered, local_kv, causal_flags))]
    select_n x7 -> x0, other arithmetic: 19.2 us -> none  [the longest x1 14.2 us: local(): picked = jnp.where(is_valid[:, None, None], picked, jnp.zeros_like(picked))]
    pallas_call x0 -> x3, Pallas kernels: none -> 16.6 us  [the longest x1 11.6 us: attend(): pl.pallas_call(functools.partial(attend_kernel, own_keys, heads), grid=(r...]
    slice x3 -> x0, local copies, waits for them, and re-layouts: 16.2 us -> none  [the longest x2 12 us: local(): arrived[:, :, 1]]
  transfers between devices with their start and end apart: 4 -> 5, of which waited for: 3 -> 5; matrix products, arithmetic and copies ran while one was open for 5% -> 3% of each run, Pallas kernels for 0% -> 3%
where the time goes in v1:
time: 187 us; the launch traced here: 186 us
  waiting for transfers between devices  93.2 us (50%)
  starting transfers between devices  40.4 us (22%)
  blocking collectives  25.5 us (14%)
  Pallas kernels  16.6 us (9%)
  local copies, waits for them, and re-layouts  10.3 us (6%)
    all_to_all x5, waiting for transfers between devices, exchange(): return lax.all_to_all(value, axes, split_axis=0, concat_axis=0, tiled=True)  93.2 us
    all_to_all x5, starting transfers between devices, exchange(): return lax.all_to_all(value, axes, split_axis=0, concat_axis=0, tiled=True)  40.4 us
    all_to_all x1, blocking collectives, exchange(): return lax.all_to_all(value, axes, split_axis=0, concat_axis=0, tiled=True)  25.5 us
    pallas_call x1, Pallas kernels, attend(): pl.pallas_call(functools.partial(attend_kernel, own_keys, heads), grid=(r...  11.6 us
    pallas_call x2, Pallas kernels, pick(): pl.pallas_call(pick_kernel, out_shape=jax.ShapeDtypeStruct((count,) + tab...  5 us
    transpose x3, local copies, waits for them, and re-layouts, spread(): mine = mine.transpose(3, 1, 0, 2, 4).reshape(ctx_size, kv_count * piece, HD)  4.41 us
  transfers between devices with their start and end apart: 5, of which 5 were waited for; matrix products, arithmetic and copies ran while one was open for 3% of the time, Pallas kernels for 3%

profile of v1, /device:TPU:2, one launch (start us, length us, event | category | flops | bytes accessed | tf_op | source)
XLA Modules:
  0.0 186.1 jit_solution(6778962527796122076)
XLA Ops:
  0.0 2.0 %dynamic-slice_bitcast_fusion = (bf16[4,32,4,8,128]{4,3,0,1,2:T(8,128)(2,1)S(1)}, bf16[4,32,4,8,128]{4,3,0,1,2:T(8,128)(2,1)S(1)}) fusion(bf16[4,512,512]{2,1,0:T(8,128)(2,1)} %param.6, s32[]{:T(128)S(6)} %select_n.4, bf16[4,512,512]{2,1,0:T(8,128)(2,1)} %param.5), kind=kLoop, calls=%fused_computation | loop fusion | bytes 4194308 | tf_op jit(solution)/shard_map/transpose | solution.py:94
  2.0 1.2 copy.29
  3.2 15.4 %all-to-all-start.1 = ((bf16[128,32,128]{2,1,0:T(8,128)(2,1)}), bf16[128,32,128]{2,1,0:T(8,128)(2,1)S(1)}, u32[]{:S(2)}, u32[]{:S(2)}) async-start(bf16[128,32,128]{2,1,0:T(8,128)(2,1)} %bitcast.6), calls=%async_computation.1 | async-start | bytes 2097152 | tf_op jit(solution)/shard_map/all_to_all | solution.py:17
  18.7 1.2 copy.31
  19.9 29.6 %all-to-all-done.1 = bf16[128,32,128]{2,1,0:T(8,128)(2,1)S(1)} async-done(((bf16[128,32,128]{2,1,0:T(8,128)(2,1)}), bf16[128,32,128]{2,1,0:T(8,128)(2,1)S(1)}, u32[]{:S(2)}, u32[]{:S(2)}) %all-to-all-start.1) | async-done | bytes 1048608 | tf_op jit(solution)/shard_map/all_to_all | solution.py:17
  49.5 6.5 %all-to-all-start.3 = ((bf16[128,32,128]{2,1,0:T(8,128)(2,1)}), bf16[128,32,128]{2,1,0:T(8,128)(2,1)S(1)}, u32[]{:S(2)}, u32[]{:S(2)}) async-start(bf16[128,32,128]{2,1,0:T(8,128)(2,1)} %bitcast.14), calls=%async_computation.3 | async-start | bytes 2097152 | tf_op jit(solution)/shard_map/all_to_all | solution.py:17
  56.2 0.6 reshape.80.index_ref
  56.9 2.5 %pick.2 = bf16[256,8,128]{2,1,0:T(8,128)(2,1)} custom-call(s32[256]{0:T(256)} %reshape.80.index_ref, bf16[512,8,128]{2,1,0:T(8,128)(2,1)} %bitcast.34), custom_call_target="tpu_custom_call" | custom-call | tf_op jit(solution)/shard_map/pick/pallas_call | solution.py:32
  59.4 26.9 %all-to-all-done.3 = bf16[128,32,128]{2,1,0:T(8,128)(2,1)S(1)} async-done(((bf16[128,32,128]{2,1,0:T(8,128)(2,1)}), bf16[128,32,128]{2,1,0:T(8,128)(2,1)S(1)}, u32[]{:S(2)}, u32[]{:S(2)}) %all-to-all-start.3) | async-done | bytes 1048608 | tf_op jit(solution)/shard_map/all_to_all | solution.py:17
  86.2 5.4 %all-to-all-start.2 = ((bf16[64,32,128]{2,1,0:T(8,128)(2,1)}), bf16[64,32,128]{2,1,0:T(8,128)(2,1)S(1)}, u32[]{:S(2)}, u32[]{:S(2)}) async-start(bf16[64,32,128]{2,1,0:T(8,128)(2,1)} %bitcast.42), calls=%async_computation.2 | async-start | bytes 1048576 | tf_op jit(solution)/shard_map/all_to_all | solution.py:17
  91.7 2.5 %pick.3 = bf16[256,8,128]{2,1,0:T(8,128)(2,1)} custom-call(s32[256]{0:T(256)} %reshape.80.index_ref, bf16[512,8,128]{2,1,0:T(8,128)(2,1)} %bitcast.35), custom_call_target="tpu_custom_call" | custom-call | tf_op jit(solution)/shard_map/pick/pallas_call | solution.py:32
  94.2 8.4 %all-to-all-done.2 = bf16[64,32,128]{2,1,0:T(8,128)(2,1)S(1)} async-done(((bf16[64,32,128]{2,1,0:T(8,128)(2,1)}), bf16[64,32,128]{2,1,0:T(8,128)(2,1)S(1)}, u32[]{:S(2)}, u32[]{:S(2)}) %all-to-all-start.2) | async-done | bytes 524320 | tf_op jit(solution)/shard_map/all_to_all | solution.py:17
  102.6 5.8 %all-to-all-start.4 = ((bf16[64,32,128]{2,1,0:T(8,128)(2,1)}), bf16[64,32,128]{2,1,0:T(8,128)(2,1)S(1)}, u32[]{:S(2)}, u32[]{:S(2)}) async-start(bf16[64,32,128]{2,1,0:T(8,128)(2,1)} %bitcast.41), calls=%async_computation.4 | async-start | bytes 1048576 | tf_op jit(solution)/shard_map/all_to_all | solution.py:17
  108.4 0.3 reshape.77
  108.8 1.0 copy.26
  109.7 9.6 %all-to-all-done.4 = bf16[64,32,128]{2,1,0:T(8,128)(2,1)S(1)} async-done(((bf16[64,32,128]{2,1,0:T(8,128)(2,1)}), bf16[64,32,128]{2,1,0:T(8,128)(2,1)S(1)}, u32[]{:S(2)}, u32[]{:S(2)}) %all-to-all-start.4) | async-done | bytes 524320 | tf_op jit(solution)/shard_map/all_to_all | solution.py:17
  119.3 7.3 %all-to-all-start = ((bf16[128,16,128]{2,1,0:T(8,128)(2,1)}), bf16[128,16,128]{2,1,0:T(8,128)(2,1)S(1)}, u32[]{:S(2)}, u32[]{:S(2)}) async-start(bf16[128,16,128]{2,1,0:T(8,128)(2,1)} %bitcast.1), calls=%async_computation | async-start | bytes 1048576 | tf_op jit(solution)/shard_map/all_to_all | solution.py:17
  126.6 0.9 copy.30
  127.5 0.9 copy.32
  128.4 18.7 %all-to-all-done = bf16[128,16,128]{2,1,0:T(8,128)(2,1)S(1)} async-done(((bf16[128,16,128]{2,1,0:T(8,128)(2,1)}), bf16[128,16,128]{2,1,0:T(8,128)(2,1)S(1)}, u32[]{:S(2)}, u32[]{:S(2)}) %all-to-all-start) | async-done | bytes 524320 | tf_op jit(solution)/shard_map/all_to_all | solution.py:17
  147.1 0.8 copy-done.2
  147.8 11.6 %attend.1 = bf16[2048,128]{1,0:T(8,128)(2,1)} custom-call(bf16[2048,128]{1,0:T(8,128)(2,1)} %bitcast.43, bf16[2048,128]{1,0:T(8,128)(2,1)} %bitcast.44, bf16[2048,128]{1,0:T(8,128)(2,1)} %bitcast.45), custom_call_target="tpu_custom_call" | custom-call | tf_op jit(solution)/shard_map/attend/pallas_call | solution.py:69
  159.4 25.5 %all_to_all.30 = bf16[128,16,128]{2,1,0:T(8,128)(2,1)S(1)} all-to-all(bf16[128,16,128]{2,1,0:T(8,128)(2,1)} %bitcast.46), channel_id=1, replica_groups=mesh['zp'=4,'zl'=2,'x'=4,'y'=4,'c'=2] {'zp','zl','x','y'}, dimensions={0} | all-to-all | bytes 1048576 | tf_op jit(solution)/shard_map/all_to_all | solution.py:17
  185.2 0.9 reshape.95
  (15 shorter events, 0.5 us)
Async XLA Ops:
  3.2 46.3 %all-to-all-start.1 = ((bf16[128,32,128]{2,1,0:T(8,128)(2,1)}), bf16[128,32,128]{2,1,0:T(8,128)(2,1)S(1)}, u32[]{:S(2)}, u32[]{:S(2)}) async-start(bf16[128,32,128]{2,1,0:T(8,128)(2,1)} %bitcast.6), calls=%async_computation.1 | async-start | bytes 2097152 | tf_op jit(solution)/shard_map/all_to_all | solution.py:17
  18.7 37.3 %copy-start.4 = (s32[64,3]{0,1:T(4,128)S(1)}, s32[64,3]{0,1:T(4,128)}, u32[]{:S(2)}) copy-start(s32[64,3]{0,1:T(4,128)} %param.7) | copy-start | bytes 2308
  49.5 7.3 %copy-start = (bf16[128,32,128]{2,1,0:T(8,128)(2,1)}, bf16[128,32,128]{2,1,0:T(8,128)(2,1)S(1)}, u32[]{:S(2)}) copy-start(bf16[128,32,128]{2,1,0:T(8,128)(2,1)S(1)} %all-to-all-done.1) | copy-start | bytes 3145732
  49.5 36.7 %all-to-all-start.3 = ((bf16[128,32,128]{2,1,0:T(8,128)(2,1)}), bf16[128,32,128]{2,1,0:T(8,128)(2,1)S(1)}, u32[]{:S(2)}, u32[]{:S(2)}) async-start(bf16[128,32,128]{2,1,0:T(8,128)(2,1)} %bitcast.14), calls=%async_computation.3 | async-start | bytes 2097152 | tf_op jit(solution)/shard_map/all_to_all | solution.py:17
  59.4 49.1 %copy-start.3 = (bf16[32,4,2048]{2,1,0:T(4,128)(2,1)S(1)}, bf16[32,4,2048]{2,1,0:T(4,128)(2,1)}, u32[]{:S(2)}) copy-start(bf16[32,4,2048]{2,1,0:T(4,128)(2,1)} %param.4) | copy-start | bytes 1572868
  86.2 5.4 %copy-start.1 = (bf16[128,32,128]{2,1,0:T(8,128)(2,1)}, bf16[128,32,128]{2,1,0:T(8,128)(2,1)S(1)}, u32[]{:S(2)}) copy-start(bf16[128,32,128]{2,1,0:T(8,128)(2,1)S(1)} %all-to-all-done.3) | copy-start | bytes 3145732
  86.2 16.4 %all-to-all-start.2 = ((bf16[64,32,128]{2,1,0:T(8,128)(2,1)}), bf16[64,32,128]{2,1,0:T(8,128)(2,1)S(1)}, u32[]{:S(2)}, u32[]{:S(2)}) async-start(bf16[64,32,128]{2,1,0:T(8,128)(2,1)} %bitcast.42), calls=%async_computation.2 | async-start | bytes 1048576 | tf_op jit(solution)/shard_map/all_to_all | solution.py:17
  102.6 16.7 %all-to-all-start.4 = ((bf16[64,32,128]{2,1,0:T(8,128)(2,1)}), bf16[64,32,128]{2,1,0:T(8,128)(2,1)S(1)}, u32[]{:S(2)}, u32[]{:S(2)}) async-start(bf16[64,32,128]{2,1,0:T(8,128)(2,1)} %bitcast.41), calls=%async_computation.4 | async-start | bytes 1048576 | tf_op jit(solution)/shard_map/all_to_all | solution.py:17
  119.3 27.7 %all-to-all-start = ((bf16[128,16,128]{2,1,0:T(8,128)(2,1)}), bf16[128,16,128]{2,1,0:T(8,128)(2,1)S(1)}, u32[]{:S(2)}, u32[]{:S(2)}) async-start(bf16[128,16,128]{2,1,0:T(8,128)(2,1)} %bitcast.1), calls=%async_computation | async-start | bytes 1048576 | tf_op jit(solution)/shard_map/all_to_all | solution.py:17
  147.0 0.8 copy-start.2

commit v2 on v1

v2 whole, which is shorter than its diff:
```python
import functools
import math

import jax
import jax.numpy as jnp
from jax import lax
from jax.experimental import pallas as pl
from jax.experimental.pallas import tpu as pltpu
from jax.sharding import Mesh, PartitionSpec as P

HD = 128
CTX = ("zp", "zl", "x", "y")
PAIR = ("zl", "x", "y", "c")


def exchange(value, axes):
    return lax.all_to_all(value, axes, split_axis=0, concat_axis=0, tiled=True)


def pick_kernel(index_ref, table_ref, out_ref):
    def body(step, carry):
        for inner in range(8):
            place = step * 8 + inner
            out_ref[place] = table_ref[index_ref[place]]
        return carry

    lax.fori_loop(0, out_ref.shape[0] // 8, body, 0)


def pick(index, table):
    count = index.shape[0]
    return pl.pallas_call(
        pick_kernel,
        out_shape=jax.ShapeDtypeStruct((count,) + table.shape[1:], table.dtype),
        in_specs=[
            pl.BlockSpec(memory_space=pltpu.SMEM),
            pl.BlockSpec(memory_space=pltpu.VMEM),
        ],
        out_specs=pl.BlockSpec(memory_space=pltpu.VMEM),
        name="pick",
    )(index, table)


def key_place(key, own_keys):
    piece, inner = key // 8, key % 8
    return (piece % 2) * (own_keys // 2) + (piece // 2) * 8 + inner


def attend_kernel(row_count, q_ref, kv_ref, out_ref, keys, values):
    sources, _, width, piece, _ = kv_ref.shape
    own_keys = sources * piece

    @pl.when(pl.program_id(0) == 0)
    def _():
        for j in range(width):
            place = pl.ds(j * own_keys, own_keys)
            keys[place] = kv_ref[:, 0, j].reshape(own_keys, HD)
            values[place] = kv_ref[:, 1, j].reshape(own_keys, HD)

    holders, rows_each, _ = q_ref.shape
    rows = holders * rows_each
    nt = (((1,), (1,)), ((), ()))
    asked = q_ref[...].reshape(rows, HD)
    scores = lax.dot_general(asked, keys[...], nt, preferred_element_type=jnp.float32)
    row = lax.broadcasted_iota(jnp.int32, (rows, 1), 0)
    token = (pl.program_id(0) * holders + row // rows_each) * row_count + row % row_count
    key = lax.broadcasted_iota(jnp.int32, (1, own_keys), 1)
    own = jnp.where(key_place(key, own_keys) <= token, scores[:, :own_keys], -jnp.inf)
    scores = jnp.concatenate([own, scores[:, own_keys:]], axis=1)
    best = jnp.max(scores, axis=1, keepdims=True)
    factor = math.log2(math.e) / math.sqrt(HD)
    weights = jnp.exp2((scores - best) * factor).astype(jnp.bfloat16)
    total = jnp.sum(weights.astype(jnp.float32), axis=1, keepdims=True)
    mixed = jnp.dot(weights, values[...], preferred_element_type=jnp.float32)
    out_ref[...] = (mixed / total).astype(out_ref.dtype).reshape(out_ref.shape)


def attend(arrived, pieces, row_count, rows_each):
    ctx_size, packed, _ = arrived.shape
    sources, _, width, piece, _ = pieces.shape
    holders = 16
    lead = packed // rows_each - 1
    return pl.pallas_call(
        functools.partial(attend_kernel, row_count),
        grid=(ctx_size // holders,),
        out_shape=jax.ShapeDtypeStruct((ctx_size, rows_each, HD), jnp.bfloat16),
        in_specs=[
            pl.BlockSpec((holders, rows_each, HD), lambda i: (i, lead, 0)),
            pl.BlockSpec(pieces.shape, lambda i: (0, 0, 0, 0, 0)),
        ],
        out_specs=pl.BlockSpec((holders, rows_each, HD), lambda i: (i, 0, 0)),
        scratch_shapes=[pltpu.VMEM((width * sources * piece, HD), jnp.bfloat16)] * 2,
        name="attend",
    )(arrived, pieces)


def local(queries, key_blocks, value_blocks, selected):
    core = lax.axis_index("c")
    half_blocks, row_count, feat_width = queries.shape
    kv_count, block, kv_width = key_blocks.shape
    groups = kv_width // HD
    heads = feat_width // kv_width
    ctx_size = lax.axis_size(CTX)
    pair_size = lax.axis_size(PAIR)
    spots = ctx_size // groups
    piece = block // pair_size

    def cut(blocks):
        mine = lax.dynamic_slice_in_dim(blocks, core * (block // 2), block // 2, 1)
        mine = mine.reshape(kv_count, spots, piece, groups, HD)
        return mine.transpose(3, 1, 0, 2, 4).reshape(ctx_size, kv_count * piece, HD)

    asked = queries.reshape(half_blocks, row_count, groups, heads, HD)
    asked = asked.transpose(2, 0, 3, 1, 4).reshape(ctx_size, heads * row_count, HD)
    parcels = jnp.concatenate([cut(key_blocks), cut(value_blocks), asked], axis=1)
    arrived = exchange(parcels, CTX)

    block_total = selected.shape[0]
    own_block = ctx_size * kv_count - block_total + jnp.arange(block_total, dtype=jnp.int32)
    targets = jnp.concatenate([own_block[:, None], selected], axis=1)
    width = targets.shape[1]
    targets = targets.reshape(2, half_blocks, 1, width).transpose(1, 0, 2, 3)
    in_parcel = parcels.shape[1] // piece
    place = targets // kv_count * in_parcel + targets % kv_count
    place = jnp.concatenate([place, place + kv_count], axis=2).reshape(-1)
    sent = pick(place, arrived.reshape(ctx_size * in_parcel, piece, HD))
    pieces = exchange(sent.reshape(pair_size, -1, HD), PAIR)
    pieces = pieces.reshape(pair_size, 2, width, piece, HD)
    done = attend(arrived, pieces, row_count, heads * row_count)
    back = exchange(done, CTX).reshape(groups, half_blocks, heads, row_count, HD)
    return back.transpose(1, 3, 0, 2, 4).reshape(queries.shape)


def solution(mesh):
    z_pairs = 4
    ctx_size, cores = mesh.devices.shape
    plane = 4
    fine = mesh.devices.reshape(z_pairs, ctx_size // (z_pairs * plane * plane), plane, plane, cores)
    fine_mesh = Mesh(fine, ("zp", "zl", "x", "y", "c"))
    in_specs = (P("c", CTX, None), P(CTX, None, None), P(CTX, None, None), P())
    out_specs = P("c", CTX, None)
    return jax.shard_map(
        local, mesh=fine_mesh, in_specs=in_specs, out_specs=out_specs, check_vma=False
    )
```

time: 187 us -> 153 us (0.82)
  waiting for transfers between devices: 93.2 us -> 62.6 us
  blocking collectives: 25.5 us -> 50.5 us
  starting transfers between devices: 40.4 us -> 15.6 us
  local copies, waits for them, and re-layouts: 10.3 us -> 7.22 us
    all_to_all x5 -> x1, waiting for transfers between devices: 93.2 us -> 62.6 us  [exchange(): return lax.all_to_all(value, axes, split_axis=0, concat_axis=0, tiled=True)]
    all_to_all x1 -> x2, blocking collectives: 25.5 us -> 50.5 us  [exchange(): return lax.all_to_all(value, axes, split_axis=0, concat_axis=0, tiled=True)]
    all_to_all x5 -> x1, starting transfers between devices: 40.4 us -> 15.6 us  [exchange(): return lax.all_to_all(value, axes, split_axis=0, concat_axis=0, tiled=True)]
    transpose x7 -> x4, local copies, waits for them, and re-layouts: 7.26 us -> 2.68 us  [the longest x3 2.4 us: cut(): return mine.transpose(3, 1, 0, 2, 4).reshape(ctx_size, kv_count * piece, HD)]
    pallas_call x2 -> x1, Pallas kernels: 5 us -> 3.64 us  [pick(): pl.pallas_call(pick_kernel, out_shape=jax.ShapeDtypeStruct((count,) + tab...]
  transfers between devices with their start and end apart: 5 -> 1, of which waited for: 5 -> 1; matrix products, arithmetic and copies ran while one was open for 3% -> 1% of each run, Pallas kernels for 3% -> 0%
where the time goes in v2:
time: 153 us
  waiting for transfers between devices  62.6 us (41%)
  blocking collectives  50.5 us (33%)
  starting transfers between devices  15.6 us (10%)
  Pallas kernels  15.1 us (10%)
  local copies, waits for them, and re-layouts  7.22 us (5%)
  other arithmetic  1.73 us (1%)
    all_to_all x1, waiting for transfers between devices, exchange(): return lax.all_to_all(value, axes, split_axis=0, concat_axis=0, tiled=True)  62.6 us
    all_to_all x2, blocking collectives, exchange(): return lax.all_to_all(value, axes, split_axis=0, concat_axis=0, tiled=True)  50.5 us
    all_to_all x1, starting transfers between devices, exchange(): return lax.all_to_all(value, axes, split_axis=0, concat_axis=0, tiled=True)  15.6 us
    pallas_call x1, Pallas kernels, attend(): pl.pallas_call(functools.partial(attend_kernel, row_count), grid=(ctx_siz...  11.5 us
    pallas_call x1, Pallas kernels, pick(): pl.pallas_call(pick_kernel, out_shape=jax.ShapeDtypeStruct((count,) + tab...  3.64 us
  transfers between devices with their start and end apart: 1, of which 1 were waited for; matrix products, arithmetic and copies ran while one was open for 1% of the time, Pallas kernels for 0%

profile of v2, /device:TPU:2, one launch (start us, length us, event | category | flops | bytes accessed | tf_op | source)
XLA Modules:
  0.0 152.8 jit_solution(13990073366267743286)
XLA Ops:
  0.0 2.0 %dynamic-slice_bitcast_fusion = (bf16[4,32,4,8,128]{4,3,0,1,2:T(8,128)(2,1)S(1)}, bf16[4,32,4,8,128]{4,3,0,1,2:T(8,128)(2,1)S(1)}) fusion(bf16[4,512,512]{2,1,0:T(8,128)(2,1)} %param.6, s32[]{:T(128)S(6)} %select_n.16, bf16[4,512,512]{2,1,0:T(8,128)(2,1)} %param.5), kind=kLoop, calls=%fused_computation.1 | loop fusion | bytes 4194308 | tf_op jit(solution)/shard_map/transpose | solution.py:111
  2.0 0.0 copy-start.1
  2.0 0.2 copy.17
  2.2 0.2 copy.18
  2.4 0.6 copy-done.1
  3.1 0.3 reshape.60
  3.4 0.2 copy.19
  3.6 1.7 %pad_maximum_fusion = bf16[128,80,128]{2,1,0:T(8,128)(2,1)} fusion(bf16[128,16,128]{2,1,0:T(8,128)(2,1)S(1)} %bitcast.31, bf16[128,32,128]{2,1,0:T(8,128)(2,1)S(1)} %bitcast.28, bf16[128,32,128]{2,1,0:T(8,128)(2,1)S(1)} %bitcast.27), kind=kLoop, calls=%fused_computation | loop fusion | flops 7864320 | bytes 5242880 | tf_op jit(solution)/shard_map/concatenate | solution.py:115
  5.3 0.0 copy-start.2
  5.3 15.6 %all-to-all-start = ((bf16[128,80,128]{2,1,0:T(8,128)(2,1)}), bf16[128,80,128]{2,1,0:T(8,128)(2,1)S(1)}, u32[]{:S(2)}, u32[]{:S(2)}) async-start(bf16[128,80,128]{2,1,0:T(8,128)(2,1)} %pad_maximum_fusion), calls=%async_computation | async-start | bytes 5242880 | tf_op jit(solution)/shard_map/all_to_all | solution.py:17
  20.9 0.0 copy-done.2
  20.9 0.1 concatenate.13
  21.0 0.1 copy.21
  21.1 0.7 reshape.62.index_ref
  21.9 62.6 %all-to-all-done.q_ref = bf16[128,80,128]{2,1,0:T(8,128)(2,1)S(1)} async-done(((bf16[128,80,128]{2,1,0:T(8,128)(2,1)}), bf16[128,80,128]{2,1,0:T(8,128)(2,1)S(1)}, u32[]{:S(2)}, u32[]{:S(2)}) %all-to-all-start) | async-done | bytes 2621472 | tf_op jit(solution)/shard_map/all_to_all | solution.py:17
  84.5 0.0 copy-start
  84.5 1.5 copy-done
  86.0 3.6 %pick.1 = bf16[512,8,128]{2,1,0:T(8,128)(2,1)} custom-call(s32[512]{0:T(512)} %reshape.62.index_ref, bf16[1280,8,128]{2,1,0:T(8,128)(2,1)} %bitcast.26), custom_call_target="tpu_custom_call" | custom-call | tf_op jit(solution)/shard_map/pick/pallas_call | solution.py:32
  89.6 22.4 %all_to_all.15 = bf16[64,64,128]{2,1,0:T(8,128)(2,1)} all-to-all(bf16[64,64,128]{2,1,0:T(8,128)(2,1)} %bitcast.29), channel_id=1, replica_groups=mesh['zp'=4,'zl'=2,'x'=4,'y'=4,'c'=2] {'zl','x','y','c'}, dimensions={0} | all-to-all | bytes 2097152 | tf_op jit(solution)/shard_map/all_to_all | solution.py:17
  112.0 11.5 %attend.1 = bf16[128,16,128]{2,1,0:T(8,128)(2,1)} custom-call(bf16[128,80,128]{2,1,0:T(8,128)(2,1)} %copy-done, bf16[64,2,4,8,128]{4,3,2,1,0:T(8,128)(2,1)} %bitcast.30), custom_call_target="tpu_custom_call" | custom-call | tf_op jit(solution)/shard_map/attend/pallas_call | solution.py:83
  123.5 28.1 %all_to_all.16 = bf16[128,16,128]{2,1,0:T(8,128)(2,1)S(1)} all-to-all(bf16[128,16,128]{2,1,0:T(8,128)(2,1)} %attend.1), channel_id=1, replica_groups=mesh['zp'=4,'zl'=2,'x'=4,'y'=4,'c'=2] {'zp','zl','x','y'}, dimensions={0} | all-to-all | bytes 1048576 | tf_op jit(solution)/shard_map/all_to_all | solution.py:17
  151.6 0.3 copy.22
  151.9 0.9 reshape.67
  (4 shorter events, 0.0 us)
Async XLA Ops:
  2.0 1.0 copy-start.1
  5.3 15.6 %copy-start.2 = (s32[64,3]{0,1:T(4,128)S(1)}, s32[64,3]{0,1:T(4,128)}, u32[]{:S(2)}) copy-start(s32[64,3]{0,1:T(4,128)} %param.7) | copy-start | bytes 2308
  5.3 79.2 %all-to-all-start = ((bf16[128,80,128]{2,1,0:T(8,128)(2,1)}), bf16[128,80,128]{2,1,0:T(8,128)(2,1)S(1)}, u32[]{:S(2)}, u32[]{:S(2)}) async-start(bf16[128,80,128]{2,1,0:T(8,128)(2,1)} %pad_maximum_fusion), calls=%async_computation | async-start | bytes 5242880 | tf_op jit(solution)/shard_map/all_to_all | solution.py:17
  84.5 1.5 copy-start

commit v3 on v2

--- a/solution.py
+++ b/solution.py
@@ -15,6 +15,47 @@
 
 def exchange(value, axes):
     return lax.all_to_all(value, axes, split_axis=0, concat_axis=0, tiled=True)
+
+
+def pack_kernel(core_ref, q_ref, k_ref, v_ref, out_ref):
+    kv_count, _, _ = k_ref.shape
+    spots, row_count, width = q_ref.shape
+    piece = k_ref.shape[1] // spots
+    at = 0
+    for ref in (k_ref, v_ref):
+        for block in range(kv_count):
+            out_ref[:, at : at + piece] = ref[block].reshape(spots, piece, HD)
+            at += piece
+    for head in range(width // HD):
+        out_ref[:, at : at + row_count] = q_ref[:, :, head * HD : (head + 1) * HD]
+        at += row_count
+
+
+def pack(core, queries, key_blocks, value_blocks):
+    kv_count, block, kv_width = key_blocks.shape
+    groups = kv_width // HD
+    half_blocks, row_count, feat_width = queries.shape
+    piece = block // 2 // half_blocks
+    tall = 2 * kv_count * piece + feat_width // kv_width * row_count
+    half = pl.BlockSpec((kv_count, block // 2, HD), lambda g, core_ref: (0, core_ref[0], g))
+    return pl.pallas_call(
+        pack_kernel,
+        grid_spec=pltpu.PrefetchScalarGridSpec(
+            num_scalar_prefetch=1,
+            grid=(groups,),
+            in_specs=[
+                pl.BlockSpec(
+                    (half_blocks, row_count, feat_width // groups),
+                    lambda g, core_ref: (0, 0, g),
+                ),
+                half,
+                half,
+            ],
+            out_specs=pl.BlockSpec((half_blocks, tall, HD), lambda g, core_ref: (g, 0, 0)),
+        ),
+        out_shape=jax.ShapeDtypeStruct((groups * half_blocks, tall, HD), queries.dtype),
+        name="pack",
+    )(core[None], queries, key_blocks, value_blocks)
 
 
 def pick_kernel(index_ref, table_ref, out_ref):
@@ -46,42 +87,69 @@
     return (piece % 2) * (own_keys // 2) + (piece // 2) * 8 + inner
 
 
-def attend_kernel(row_count, q_ref, kv_ref, out_ref, keys, values):
+def attend_kernel(row_count, parts, q_ref, kv_ref, out_ref, keys, values):
     sources, _, width, piece, _ = kv_ref.shape
     own_keys = sources * piece
+    holders, rows_each, _ = q_ref.shape
+    holders = holders // parts
+    rows = holders * rows_each
+    factor = math.log2(math.e) / math.sqrt(HD)
+    nt = (((1,), (1,)), ((), ()))
 
     @pl.when(pl.program_id(0) == 0)
     def _():
         for j in range(width):
             place = pl.ds(j * own_keys, own_keys)
             keys[place] = kv_ref[:, 0, j].reshape(own_keys, HD)
-            values[place] = kv_ref[:, 1, j].reshape(own_keys, HD)
-
-    holders, rows_each, _ = q_ref.shape
-    rows = holders * rows_each
-    nt = (((1,), (1,)), ((), ()))
-    asked = q_ref[...].reshape(rows, HD)
-    scores = lax.dot_general(asked, keys[...], nt, preferred_element_type=jnp.float32)
-    row = lax.broadcasted_iota(jnp.int32, (rows, 1), 0)
-    token = (pl.program_id(0) * holders + row // rows_each) * row_count + row % row_count
-    key = lax.broadcasted_iota(jnp.int32, (1, own_keys), 1)
-    own = jnp.where(key_place(key, own_keys) <= token, scores[:, :own_keys], -jnp.inf)
-    scores = jnp.concatenate([own, scores[:, own_keys:]], axis=1)
-    best = jnp.max(scores, axis=1, keepdims=True)
-    factor = math.log2(math.e) / math.sqrt(HD)
-    weights = jnp.exp2((scores - best) * factor).astype(jnp.bfloat16)
-    total = jnp.sum(weights.astype(jnp.float32), axis=1, keepdims=True)
-    mixed = jnp.dot(weights, values[...], preferred_element_type=jnp.float32)
-    out_ref[...] = (mixed / total).astype(out_ref.dtype).reshape(out_ref.shape)
+            values[place, :HD] = kv_ref[:, 1, j].reshape(own_keys, HD)
+        values[:, HD:] = jnp.ones((width * own_keys, HD), jnp.bfloat16)
+
+    def steps(part):
+        held = pl.ds(part * holders, holders)
+        asked = q_ref[held].reshape(rows, HD)
+        scores = [
+            lax.dot_general(
+                asked,
+                keys[pl.ds(j * own_keys, own_keys)],
+                nt,
+                preferred_element_type=jnp.float32,
+            )
+            for j in range(width)
+        ]
+        row = lax.broadcasted_iota(jnp.int32, (rows, 1), 0)
+        holder = (pl.program_id(0) * parts + part) * holders + row // rows_each
+        token = holder * row_count + row % row_count
+        key = lax.broadcasted_iota(jnp.int32, (1, own_keys), 1)
+        scores[0] = jnp.where(key_place(key, own_keys) <= token, scores[0], -jnp.inf)
+        yield
+        best = functools.reduce(jnp.maximum, scores)
+        best = jnp.max(best, axis=1, keepdims=True)
+        yield
+        mixed = jnp.zeros((rows, 2 * HD), jnp.float32)
+        for j in range(width):
+            weights = jnp.exp2((scores[j] - best) * factor).astype(jnp.bfloat16)
+            mixed += jnp.dot(
+                weights,
+                values[pl.ds(j * own_keys, own_keys)],
+                preferred_element_type=jnp.float32,
+            )
+        result = mixed[:, :HD] / mixed[:, HD:]
+        out_ref[held] = result.astype(out_ref.dtype).reshape(holders, rows_each, HD)
+        yield
+
+    running = [steps(part) for part in range(parts)]
+    for _ in range(3):
+        for one in running:
+            next(one)
 
 
 def attend(arrived, pieces, row_count, rows_each):
     ctx_size, packed, _ = arrived.shape
     sources, _, width, piece, _ = pieces.shape
-    holders = 16
+    holders, parts = 64, 4
     lead = packed // rows_each - 1
     return pl.pallas_call(
-        functools.partial(attend_kernel, row_count),
+        functools.partial(attend_kernel, row_count, parts),
         grid=(ctx_size // holders,),
         out_shape=jax.ShapeDtypeStruct((ctx_size, rows_each, HD), jnp.bfloat16),
         in_specs=[
@@ -89,7 +157,10 @@
             pl.BlockSpec(pieces.shape, lambda i: (0, 0, 0, 0, 0)),
         ],
         out_specs=pl.BlockSpec((holders, rows_each, HD), lambda i: (i, 0, 0)),
-        scratch_shapes=[pltpu.VMEM((width * sources * piece, HD), jnp.bfloat16)] * 2,
+        scratch_shapes=[
+            pltpu.VMEM((width * sources * piece, HD), jnp.bfloat16),
+            pltpu.VMEM((width * sources * piece, 2 * HD), jnp.bfloat16),
+        ],
         name="attend",
     )(arrived, pieces)
 
@@ -102,17 +173,8 @@
     heads = feat_width // kv_width
     ctx_size = lax.axis_size(CTX)
     pair_size = lax.axis_size(PAIR)
-    spots = ctx_size // groups
     piece = block // pair_size
-
-    def cut(blocks):
-        mine = lax.dynamic_slice_in_dim(blocks, core * (block // 2), block // 2, 1)
-        mine = mine.reshape(kv_count, spots, piece, groups, HD)
-        return mine.transpose(3, 1, 0, 2, 4).reshape(ctx_size, kv_count * piece, HD)
-
-    asked = queries.reshape(half_blocks, row_count, groups, heads, HD)
-    asked = asked.transpose(2, 0, 3, 1, 4).reshape(ctx_size, heads * row_count, HD)
-    parcels = jnp.concatenate([cut(key_blocks), cut(value_blocks), asked], axis=1)
+    parcels = pack(core, queries, key_blocks, value_blocks)
     arrived = exchange(parcels, CTX)
 
     block_total = selected.shape[0]
@@ -123,7 +185,8 @@
     in_parcel = parcels.shape[1] // piece
     place = targets // kv_count * in_parcel + targets % kv_count
     place = jnp.concatenate([place, place + kv_count], axis=2).reshape(-1)
-    sent = pick(place, arrived.reshape(ctx_size * in_parcel, piece, HD))
+    table = arrived.reshape(ctx_size * in_parcel, piece, HD)
+    sent = pick(place, pltpu.with_memory_space_constraint(table, pltpu.VMEM))
     pieces = exchange(sent.reshape(pair_size, -1, HD), PAIR)
     pieces = pieces.reshape(pair_size, 2, width, piece, HD)
     done = attend(arrived, pieces, row_count, heads * row_count)

time: 153 us -> 145 us (0.948)
  local copies, waits for them, and re-layouts: 7.22 us -> 2.13 us
  other arithmetic: 1.73 us -> 0.03 us
    transpose x3 -> x0, local copies, waits for them, and re-layouts: 2.4 us -> none  [cut(): return mine.transpose(3, 1, 0, 2, 4).reshape(ctx_size, kv_count * piece, HD)]
    unnamed x6 -> x4, local copies, waits for them, and re-layouts: 2.15 us -> 0.01 us
    concatenate x1 -> x0, other arithmetic: 1.69 us -> none  [local(): jnp.concatenate([cut(key_blocks), cut(value_blocks), asked], axis=1)]
    pallas_call x1 -> x2, Pallas kernels: 11.5 us -> 11.5 us  [the longest x1 7.26 us: attend(): pl.pallas_call(functools.partial(attend_kernel, row_count, parts), grid=(...]
where the time goes in v3:
time: 145 us
  waiting for transfers between devices  62.6 us (43%)
  blocking collectives  50.5 us (35%)
  starting transfers between devices  15.6 us (11%)
  Pallas kernels  14.1 us (10%)
  local copies, waits for them, and re-layouts  2.13 us (1%)
    all_to_all x1, waiting for transfers between devices, exchange(): return lax.all_to_all(value, axes, split_axis=0, concat_axis=0, tiled=True)  62.6 us
    all_to_all x2, blocking collectives, exchange(): return lax.all_to_all(value, axes, split_axis=0, concat_axis=0, tiled=True)  50.5 us
    all_to_all x1, starting transfers between devices, exchange(): return lax.all_to_all(value, axes, split_axis=0, concat_axis=0, tiled=True)  15.6 us
    pallas_call x1, Pallas kernels, attend(): pl.pallas_call(functools.partial(attend_kernel, row_count, parts), grid=(...  7.26 us
    pallas_call x1, Pallas kernels, pack(): pl.pallas_call(pack_kernel, grid_spec=pltpu.PrefetchScalarGridSpec(num_sc...  4.27 us
  transfers between devices with their start and end apart: 1, of which 1 were waited for; matrix products, arithmetic and copies ran while one was open for 1% of the time, Pallas kernels for 0%

profile of v3, /device:TPU:2, one launch (start us, length us, event | category | flops | bytes accessed | tf_op | source)
XLA Modules:
  0.0 145.0 jit_solution(12063544385164350889)
XLA Ops:
  0.0 4.3 %pack.1 = bf16[128,80,128]{2,1,0:T(8,128)(2,1)} custom-call(s32[1]{0:T(128)} %bitcast.core_ref, bf16[32,4,2048]{2,1,0:T(4,128)(2,1)} %q_ref.1, bf16[4,512,512]{2,1,0:T(8,128)(2,1)} %k_ref.1, bf16[4,512,512]{2,1,0:T(8,128)(2,1)} %v_ref.1), custom_call_target="tpu_custom_call" | custom-call | tf_op jit(solution)/shard_map/pack/pallas_call | solution.py:41
  4.3 0.0 copy-start.1
  4.3 15.6 %all-to-all-start = ((bf16[128,80,128]{2,1,0:T(8,128)(2,1)}), bf16[128,80,128]{2,1,0:T(8,128)(2,1)S(1)}, u32[]{:S(2)}, u32[]{:S(2)}) async-start(bf16[128,80,128]{2,1,0:T(8,128)(2,1)} %pack.1), calls=%async_computation | async-start | bytes 5242880 | tf_op jit(solution)/shard_map/all_to_all | solution.py:17
  19.8 0.0 copy-done.1
  19.9 0.1 concatenate.9
  20.0 0.1 copy.11
  20.1 0.7 reshape.38.index_ref
  20.8 62.6 %all-to-all-done.q_ref = bf16[128,80,128]{2,1,0:T(8,128)(2,1)S(1)} async-done(((bf16[128,80,128]{2,1,0:T(8,128)(2,1)}), bf16[128,80,128]{2,1,0:T(8,128)(2,1)S(1)}, u32[]{:S(2)}, u32[]{:S(2)}) %all-to-all-start) | async-done | bytes 2621472 | tf_op jit(solution)/shard_map/all_to_all | solution.py:17
  83.4 0.0 copy-start
  83.4 2.6 %pick.1 = bf16[512,8,128]{2,1,0:T(8,128)(2,1)} custom-call(s32[512]{0:T(512)} %reshape.38.index_ref, bf16[1280,8,128]{2,1,0:T(8,128)(2,1)S(1)} %bitcast.14), custom_call_target="tpu_custom_call" | custom-call | tf_op jit(solution)/shard_map/pick/pallas_call | solution.py:73
  86.0 22.4 %all_to_all.15 = bf16[64,64,128]{2,1,0:T(8,128)(2,1)} all-to-all(bf16[64,64,128]{2,1,0:T(8,128)(2,1)} %bitcast.15), channel_id=1, replica_groups=mesh['zp'=4,'zl'=2,'x'=4,'y'=4,'c'=2] {'zl','x','y','c'}, dimensions={0} | all-to-all | bytes 2097152 | tf_op jit(solution)/shard_map/all_to_all | solution.py:17
  108.4 0.0 copy-done
  108.4 7.3 %attend.1 = bf16[128,16,128]{2,1,0:T(8,128)(2,1)} custom-call(bf16[128,80,128]{2,1,0:T(8,128)(2,1)} %copy-done, bf16[64,2,4,8,128]{4,3,2,1,0:T(8,128)(2,1)} %bitcast.16), custom_call_target="tpu_custom_call" | custom-call | tf_op jit(solution)/shard_map/attend/pallas_call | solution.py:151
  115.7 28.1 %all_to_all.16 = bf16[128,16,128]{2,1,0:T(8,128)(2,1)S(1)} all-to-all(bf16[128,16,128]{2,1,0:T(8,128)(2,1)} %attend.1), channel_id=1, replica_groups=mesh['zp'=4,'zl'=2,'x'=4,'y'=4,'c'=2] {'zp','zl','x','y'}, dimensions={0} | all-to-all | bytes 1048576 | tf_op jit(solution)/shard_map/all_to_all | solution.py:17
  143.8 0.3 copy.12
  144.1 0.9 reshape.43
  (4 shorter events, 0.0 us)
Async XLA Ops:
  4.3 15.6 %copy-start.1 = (s32[64,3]{0,1:T(4,128)S(1)}, s32[64,3]{0,1:T(4,128)}, u32[]{:S(2)}) copy-start(s32[64,3]{0,1:T(4,128)} %param.7) | copy-start | bytes 2308
  4.3 79.2 %all-to-all-start = ((bf16[128,80,128]{2,1,0:T(8,128)(2,1)}), bf16[128,80,128]{2,1,0:T(8,128)(2,1)S(1)}, u32[]{:S(2)}, u32[]{:S(2)}) async-start(bf16[128,80,128]{2,1,0:T(8,128)(2,1)} %pack.1), calls=%async_computation | async-start | bytes 5242880 | tf_op jit(solution)/shard_map/all_to_all | solution.py:17
  83.4 25.0 %copy-start = (bf16[128,80,128]{2,1,0:T(8,128)(2,1)}, bf16[128,80,128]{2,1,0:T(8,128)(2,1)S(1)}, u32[]{:S(2)}) copy-start(bf16[128,80,128]{2,1,0:T(8,128)(2,1)S(1)} %all-to-all-done.q_ref) | copy-start | bytes 7864324

commit v4 on v3

v4 whole, which is shorter than its diff:
```python
import functools
import math

import jax
import jax.numpy as jnp
from jax import lax
from jax.experimental import pallas as pl
from jax.experimental.pallas import tpu as pltpu
from jax.sharding import Mesh, PartitionSpec as P

HD = 128
CTX = ("zp", "zl", "x", "y")
PAIR = ("zl", "x", "y", "c")


def exchange(value, axes):
    return lax.all_to_all(value, axes, split_axis=0, concat_axis=0, tiled=True)


def pack_kernel(core_ref, q_ref, k_ref, v_ref, out_ref, held, in_sems, out_sems):
    kv_count, spots, piece, kv_width = k_ref.shape
    _, row_count, feat_width = q_ref.shape
    groups = kv_width // HD
    heads = feat_width // kv_width

    def fetch(ref, g, one):
        return pltpu.make_async_copy(
            ref.at[one, :, :, pl.ds(g * HD, HD)],
            held.at[pl.ds(g * spots, spots), pl.ds(one * piece, piece)],
            in_sems.at[g, one],
        )

    def leave(g):
        part = pl.ds(g * spots, spots)
        return pltpu.make_async_copy(held.at[part], out_ref.at[part], out_sems.at[g])

    for core, ref in enumerate((k_ref, v_ref)):

        @pl.when(core_ref[0] == core)
        def _():
            for g in range(groups):
                for one in range(kv_count):
                    fetch(ref, g, one).start()

    for g in range(groups):
        for head in range(heads):
            rows = pl.ds(kv_count * piece + head * row_count, row_count)
            at = (g * heads + head) * HD
            held[pl.ds(g * spots, spots), rows] = q_ref[:, :, at : at + HD]
    for g in range(groups):
        for one in range(kv_count):
            fetch(k_ref, g, one).wait()
        leave(g).start()
    for g in range(groups):
        leave(g).wait()


def pack(core, queries, key_blocks, value_blocks):
    kv_count, block, kv_width = key_blocks.shape
    groups = kv_width // HD
    half_blocks, row_count, feat_width = queries.shape
    piece = block // half_blocks
    tall = kv_count * piece + feat_width // kv_width * row_count
    whole = jax.ShapeDtypeStruct((groups * half_blocks, tall, HD), queries.dtype)
    cut = (kv_count, half_blocks, piece, kv_width)
    away = pl.BlockSpec(memory_space=pl.ANY)
    return pl.pallas_call(
        pack_kernel,
        out_shape=whole,
        in_specs=[
            pl.BlockSpec(memory_space=pltpu.SMEM),
            pl.BlockSpec(memory_space=pltpu.VMEM),
            away,
            away,
        ],
        out_specs=away,
        scratch_shapes=[
            pltpu.VMEM(whole.shape, whole.dtype),
            pltpu.SemaphoreType.DMA((groups, kv_count)),
            pltpu.SemaphoreType.DMA((groups,)),
        ],
        name="pack",
    )(core[None], queries, key_blocks.reshape(cut), value_blocks.reshape(cut))


def pick_kernel(index_ref, table_ref, out_ref):
    def body(step, carry):
        for inner in range(8):
            place = step * 8 + inner
            out_ref[place] = table_ref[index_ref[place]]
        return carry

    lax.fori_loop(0, out_ref.shape[0] // 8, body, 0)


def pick(index, table):
    count = index.shape[0]
    return pl.pallas_call(
        pick_kernel,
        out_shape=jax.ShapeDtypeStruct((count,) + table.shape[1:], table.dtype),
        in_specs=[
            pl.BlockSpec(memory_space=pltpu.SMEM),
            pl.BlockSpec(memory_space=pltpu.VMEM),
        ],
        out_specs=pl.BlockSpec(memory_space=pltpu.VMEM),
        name="pick",
    )(index, table)


def attend_kernel(row_count, parts, q_ref, kv_ref, out_ref, keys, values):
    spots, _, width, piece, _ = kv_ref.shape
    own_keys = spots * piece
    ctx_size, rows_each, _ = q_ref.shape
    holders = ctx_size // parts
    rows = holders * rows_each
    factor = math.log2(math.e) / math.sqrt(HD)
    nt = (((1,), (1,)), ((), ()))
    for j in range(width):
        place = pl.ds(j * own_keys, own_keys)
        keys[place] = kv_ref[:, 0, j].reshape(own_keys, HD)
        values[place, :HD] = kv_ref[:, 1, j].reshape(own_keys, HD)
    values[:, HD:] = jnp.ones((width * own_keys, HD), jnp.bfloat16)

    def steps(part):
        held = pl.ds(part * holders, holders)
        asked = q_ref[held].reshape(rows, HD)
        seen = min(own_keys, -(-(part + 1) * holders * row_count // 128) * 128)
        spans = [(0, seen)] + [(j * own_keys, own_keys) for j in range(1, width)]
        scores = [
            lax.dot_general(asked, keys[pl.ds(*span)], nt, preferred_element_type=jnp.float32)
            for span in spans
        ]
        row = lax.broadcasted_iota(jnp.int32, (rows, 1), 0)
        token = (part * holders + row // rows_each) * row_count + row % row_count
        key = lax.broadcasted_iota(jnp.int32, (1, seen), 1)
        scores[0] = jnp.where(key <= token, scores[0], -jnp.inf)
        yield
        best = functools.reduce(jnp.maximum, [jnp.max(s, axis=1, keepdims=True) for s in scores])
        yield
        mixed = jnp.zeros((rows, 2 * HD), jnp.float32)
        for score, span in zip(scores, spans):
            weights = jnp.exp2((score - best) * factor).astype(jnp.bfloat16)
            mixed += jnp.dot(weights, values[pl.ds(*span)], preferred_element_type=jnp.float32)
        result = mixed[:, :HD] / mixed[:, HD:]
        out_ref[held] = result.astype(out_ref.dtype).reshape(holders, rows_each, HD)
        yield

    running = [steps(part) for part in range(parts)]
    for _ in range(3):
        for one in running:
            next(one)


def attend(arrived, pieces, row_count, rows_each):
    ctx_size, packed, _ = arrived.shape
    spots, _, width, piece, _ = pieces.shape
    parts = 8
    lead = packed // rows_each - 1
    return pl.pallas_call(
        functools.partial(attend_kernel, row_count, parts),
        grid=(1,),
        out_shape=jax.ShapeDtypeStruct((ctx_size, rows_each, HD), jnp.bfloat16),
        in_specs=[
            pl.BlockSpec((ctx_size, rows_each, HD), lambda i: (0, lead, 0)),
            pl.BlockSpec(pieces.shape, lambda i: (0, 0, 0, 0, 0)),
        ],
        out_specs=pl.BlockSpec((ctx_size, rows_each, HD), lambda i: (0, 0, 0)),
        scratch_shapes=[
            pltpu.VMEM((width * spots * piece, HD), jnp.bfloat16),
            pltpu.VMEM((width * spots * piece, 2 * HD), jnp.bfloat16),
        ],
        name="attend",
    )(arrived, pieces)


def local(queries, key_blocks, value_blocks, selected):
    core = lax.axis_index("c")
    half_blocks, row_count, feat_width = queries.shape
    kv_count, block, kv_width = key_blocks.shape
    groups = kv_width // HD
    heads = feat_width // kv_width
    ctx_size = lax.axis_size(CTX)
    pair_size = lax.axis_size(PAIR)
    piece = block // half_blocks
    parcels = pack(core, queries, key_blocks, value_blocks)
    arrived = exchange(parcels, CTX)

    block_total = selected.shape[0]
    own_block = ctx_size * kv_count - block_total + jnp.arange(block_total, dtype=jnp.int32)
    targets = jnp.concatenate([own_block[:, None], selected], axis=1)
    width = targets.shape[1]
    targets = targets.reshape(2, half_blocks, width).transpose(1, 0, 2).reshape(-1)
    in_parcel = parcels.shape[1] // piece
    place = targets // kv_count * in_parcel + targets % kv_count
    table = arrived.reshape(ctx_size * in_parcel, piece, HD)
    sent = pick(place, pltpu.with_memory_space_constraint(table, pltpu.VMEM))
    pieces = exchange(sent.reshape(pair_size, width * piece, HD), PAIR)
    pieces = pieces.reshape(half_blocks, 2, width, piece, HD)
    done = attend(arrived, pieces, row_count, heads * row_count)
    back = exchange(done, CTX).reshape(groups, half_blocks, heads, row_count, HD)
    return back.transpose(1, 3, 0, 2, 4).reshape(queries.shape)


def solution(mesh):
    z_pairs = 4
    ctx_size, cores = mesh.devices.shape
    plane = 4
    fine = mesh.devices.reshape(z_pairs, ctx_size // (z_pairs * plane * plane), plane, plane, cores)
    fine_mesh = Mesh(fine, ("zp", "zl", "x", "y", "c"))
    in_specs = (P("c", CTX, None), P(CTX, None, None), P(CTX, None, None), P())
    out_specs = P("c", CTX, None)
    return jax.shard_map(
        local, mesh=fine_mesh, in_specs=in_specs, out_specs=out_specs, check_vma=False
    )
```

time: 145 us -> 144 us (level)
  no operation moved by 1% of the time
where the time goes in v4:
time: 144 us
  waiting for transfers between devices  62.7 us (44%)
  blocking collectives  50.5 us (35%)
  starting transfers between devices  15.4 us (11%)
  Pallas kernels  12.7 us (9%)
  local copies, waits for them, and re-layouts  1.52 us (1%)
    all_to_all x1, waiting for transfers between devices, exchange(): return lax.all_to_all(value, axes, split_axis=0, concat_axis=0, tiled=True)  62.7 us
    all_to_all x2, blocking collectives, exchange(): return lax.all_to_all(value, axes, split_axis=0, concat_axis=0, tiled=True)  50.5 us
    all_to_all x1, starting transfers between devices, exchange(): return lax.all_to_all(value, axes, split_axis=0, concat_axis=0, tiled=True)  15.4 us
    pallas_call x1, Pallas kernels, attend(): pl.pallas_call(functools.partial(attend_kernel, row_count, parts), grid=(...  6.77 us
    pallas_call x1, Pallas kernels, pack(): pl.pallas_call(pack_kernel, out_shape=whole, in_specs=[pl.BlockSpec(memor...  3.84 us
  transfers between devices with their start and end apart: 1, of which 1 were waited for; matrix products, arithmetic and copies ran while one was open for 1% of the time, Pallas kernels for 0%

profile of v4, /device:TPU:2, one launch (start us, length us, event | category | flops | bytes accessed | tf_op | source)
XLA Modules:
  0.0 143.5 jit_solution(14950938794858387323)
XLA Ops:
  0.0 3.8 %pack.1 = bf16[128,80,128]{2,1,0:T(8,128)(2,1)} custom-call(s32[1]{0:T(128)} %bitcast.core_ref, bf16[32,4,2048]{2,1,0:T(4,128)(2,1)} %q_ref.1, bf16[4,32,16,512]{3,2,1,0:T(8,128)(2,1)} %bitcast.17, bf16[4,32,16,512]{3,2,1,0:T(8,128)(2,1)} %bitcast.18), custom_call_target="tpu_custom_call" | custom-call | tf_op jit(solution)/shard_map/pack/pallas_call | solution.py:67
  3.8 0.0 copy-start.1
  3.9 15.4 %all-to-all-start = ((bf16[128,80,128]{2,1,0:T(8,128)(2,1)}), bf16[128,80,128]{2,1,0:T(8,128)(2,1)S(1)}, u32[]{:S(2)}, u32[]{:S(2)}) async-start(bf16[128,80,128]{2,1,0:T(8,128)(2,1)} %pack.1), calls=%async_computation | async-start | bytes 5242880 | tf_op jit(solution)/shard_map/all_to_all | solution.py:17
  19.3 0.0 copy-done.1
  19.3 0.1 concatenate.6
  19.4 0.1 copy.11
  19.5 0.1 reshape.46
  19.6 0.6 fusion.index_ref
  20.2 62.7 %all-to-all-done.q_ref = bf16[128,80,128]{2,1,0:T(8,128)(2,1)S(1)} async-done(((bf16[128,80,128]{2,1,0:T(8,128)(2,1)}), bf16[128,80,128]{2,1,0:T(8,128)(2,1)S(1)}, u32[]{:S(2)}, u32[]{:S(2)}) %all-to-all-start) | async-done | bytes 2621472 | tf_op jit(solution)/shard_map/all_to_all | solution.py:17
  82.9 0.0 copy-start
  82.9 2.1 %pick.1 = bf16[256,16,128]{2,1,0:T(8,128)(2,1)} custom-call(s32[256]{0:T(256)} %fusion.index_ref, bf16[640,16,128]{2,1,0:T(8,128)(2,1)S(1)} %bitcast.13), custom_call_target="tpu_custom_call" | custom-call | tf_op jit(solution)/shard_map/pick/pallas_call | solution.py:98
  85.0 22.4 %all_to_all.15 = bf16[64,64,128]{2,1,0:T(8,128)(2,1)} all-to-all(bf16[64,64,128]{2,1,0:T(8,128)(2,1)} %bitcast.15), channel_id=1, replica_groups=mesh['zp'=4,'zl'=2,'x'=4,'y'=4,'c'=2] {'zl','x','y','c'}, dimensions={0} | all-to-all | bytes 2097152 | tf_op jit(solution)/shard_map/all_to_all | solution.py:17
  107.4 0.0 copy-done
  107.4 6.8 %attend.1 = bf16[128,16,128]{2,1,0:T(8,128)(2,1)} custom-call(bf16[128,80,128]{2,1,0:T(8,128)(2,1)} %copy-done, bf16[32,2,4,16,128]{4,3,2,1,0:T(8,128)(2,1)} %bitcast.14), custom_call_target="tpu_custom_call" | custom-call | tf_op jit(solution)/shard_map/attend/pallas_call | solution.py:159
  114.2 28.1 %all_to_all.16 = bf16[128,16,128]{2,1,0:T(8,128)(2,1)S(1)} all-to-all(bf16[128,16,128]{2,1,0:T(8,128)(2,1)} %attend.1), channel_id=1, replica_groups=mesh['zp'=4,'zl'=2,'x'=4,'y'=4,'c'=2] {'zp','zl','x','y'}, dimensions={0} | all-to-all | bytes 1048576 | tf_op jit(solution)/shard_map/all_to_all | solution.py:17
  142.3 0.3 copy.12
  142.6 0.9 reshape.51
  (3 shorter events, 0.0 us)
Async XLA Ops:
  3.8 15.5 %copy-start.1 = (s32[64,3]{0,1:T(4,128)S(1)}, s32[64,3]{0,1:T(4,128)}, u32[]{:S(2)}) copy-start(s32[64,3]{0,1:T(4,128)} %param.7) | copy-start | bytes 2308
  3.9 79.0 %all-to-all-start = ((bf16[128,80,128]{2,1,0:T(8,128)(2,1)}), bf16[128,80,128]{2,1,0:T(8,128)(2,1)S(1)}, u32[]{:S(2)}, u32[]{:S(2)}) async-start(bf16[128,80,128]{2,1,0:T(8,128)(2,1)} %pack.1), calls=%async_computation | async-start | bytes 5242880 | tf_op jit(solution)/shard_map/all_to_all | solution.py:17
  82.9 24.5 %copy-start = (bf16[128,80,128]{2,1,0:T(8,128)(2,1)}, bf16[128,80,128]{2,1,0:T(8,128)(2,1)S(1)}, u32[]{:S(2)}) copy-start(bf16[128,80,128]{2,1,0:T(8,128)(2,1)S(1)} %all-to-all-done.q_ref) | copy-start | bytes 7864324

commit v5 on v4

--- a/solution.py
+++ b/solution.py
@@ -17,7 +17,7 @@
     return lax.all_to_all(value, axes, split_axis=0, concat_axis=0, tiled=True)
 
 
-def pack_kernel(core_ref, q_ref, k_ref, v_ref, out_ref, held, in_sems, out_sems):
+def pack_kernel(core_ref, q_ref, k_ref, v_ref, out_ref, asked, held, q_sem, in_sems, out_sems):
     kv_count, spots, piece, kv_width = k_ref.shape
     _, row_count, feat_width = q_ref.shape
     groups = kv_width // HD
@@ -34,6 +34,8 @@
         part = pl.ds(g * spots, spots)
         return pltpu.make_async_copy(held.at[part], out_ref.at[part], out_sems.at[g])
 
+    whole = pltpu.make_async_copy(q_ref, asked, q_sem)
+    whole.start()
     for core, ref in enumerate((k_ref, v_ref)):
 
         @pl.when(core_ref[0] == core)
@@ -42,11 +44,12 @@
                 for one in range(kv_count):
                     fetch(ref, g, one).start()
 
+    whole.wait()
     for g in range(groups):
         for head in range(heads):
             rows = pl.ds(kv_count * piece + head * row_count, row_count)
             at = (g * heads + head) * HD
-            held[pl.ds(g * spots, spots), rows] = q_ref[:, :, at : at + HD]
+            held[pl.ds(g * spots, spots), rows] = asked[:, :, at : at + HD]
     for g in range(groups):
         for one in range(kv_count):
             fetch(k_ref, g, one).wait()
@@ -69,13 +72,15 @@
         out_shape=whole,
         in_specs=[
             pl.BlockSpec(memory_space=pltpu.SMEM),
-            pl.BlockSpec(memory_space=pltpu.VMEM),
             away,
             away,
+            away,
         ],
         out_specs=away,
         scratch_shapes=[
+            pltpu.VMEM(queries.shape, queries.dtype),
             pltpu.VMEM(whole.shape, whole.dtype),
+            pltpu.SemaphoreType.DMA(()),
             pltpu.SemaphoreType.DMA((groups, kv_count)),
             pltpu.SemaphoreType.DMA((groups,)),
         ],
@@ -107,10 +112,11 @@
     )(index, table)
 
 
-def attend_kernel(row_count, parts, q_ref, kv_ref, out_ref, keys, values):
+def attend_kernel(row_count, parts, q_ref, kv_ref, out_ref, keys, values, ready, sems):
     spots, _, width, piece, _ = kv_ref.shape
     own_keys = spots * piece
-    ctx_size, rows_each, _ = q_ref.shape
+    ctx_size, rows_each, _ = out_ref.shape
+    lead = q_ref.shape[1] - rows_each
     holders = ctx_size // parts
     rows = holders * rows_each
     factor = math.log2(math.e) / math.sqrt(HD)
@@ -123,7 +129,7 @@
 
     def steps(part):
         held = pl.ds(part * holders, holders)
-        asked = q_ref[held].reshape(rows, HD)
+        asked = q_ref[held, lead:].reshape(rows, HD)
         seen = min(own_keys, -(-(part + 1) * holders * row_count // 128) * 128)
         spans = [(0, seen)] + [(j * own_keys, own_keys) for j in range(1, width)]
         scores = [
@@ -142,35 +148,66 @@
             weights = jnp.exp2((score - best) * factor).astype(jnp.bfloat16)
             mixed += jnp.dot(weights, values[pl.ds(*span)], preferred_element_type=jnp.float32)
         result = mixed[:, :HD] / mixed[:, HD:]
-        out_ref[held] = result.astype(out_ref.dtype).reshape(holders, rows_each, HD)
+        ready[held] = result.astype(out_ref.dtype).reshape(holders, rows_each, HD)
+        leave(part).start()
         yield
+
+    def leave(part):
+        held = pl.ds(part * holders, holders)
+        return pltpu.make_async_copy(ready.at[held], out_ref.at[held], sems.at[part])
 
     running = [steps(part) for part in range(parts)]
     for _ in range(3):
         for one in running:
             next(one)
+    for part in range(parts):
+        leave(part).wait()
 
 
 def attend(arrived, pieces, row_count, rows_each):
-    ctx_size, packed, _ = arrived.shape
+    ctx_size = arrived.shape[0]
     spots, _, width, piece, _ = pieces.shape
     parts = 8
-    lead = packed // rows_each - 1
+    whole = jax.ShapeDtypeStruct((ctx_size, rows_each, HD), jnp.bfloat16)
+    near = pl.BlockSpec(memory_space=pltpu.VMEM)
     return pl.pallas_call(
         functools.partial(attend_kernel, row_count, parts),
-        grid=(1,),
-        out_shape=jax.ShapeDtypeStruct((ctx_size, rows_each, HD), jnp.bfloat16),
-        in_specs=[
-            pl.BlockSpec((ctx_size, rows_each, HD), lambda i: (0, lead, 0)),
-            pl.BlockSpec(pieces.shape, lambda i: (0, 0, 0, 0, 0)),
-        ],
-        out_specs=pl.BlockSpec((ctx_size, rows_each, HD), lambda i: (0, 0, 0)),
+        out_shape=whole,
+        in_specs=[near, near],
+        out_specs=pl.BlockSpec(memory_space=pl.ANY),
         scratch_shapes=[
             pltpu.VMEM((width * spots * piece, HD), jnp.bfloat16),
             pltpu.VMEM((width * spots * piece, 2 * HD), jnp.bfloat16),
-        ],
+            pltpu.VMEM(whole.shape, whole.dtype),
+            pltpu.SemaphoreType.DMA((parts,)),
+        ],
+        compiler_params=pltpu.CompilerParams(vmem_limit_bytes=48 * 2**20),
         name="attend",
-    )(arrived, pieces)
+    )(
+        pltpu.with_memory_space_constraint(arrived, pltpu.VMEM),
+        pltpu.with_memory_space_constraint(pieces, pltpu.VMEM),
+    )
+
+
+def unpack_kernel(back_ref, out_ref):
+    spots, row_count, feat_width = out_ref.shape
+    heads = back_ref.shape[1] // row_count
+    for g in range(back_ref.shape[0] // spots):
+        for head in range(heads):
+            at = (g * heads + head) * HD
+            rows = pl.ds(head * row_count, row_count)
+            out_ref[:, :, at : at + HD] = back_ref[g * spots : (g + 1) * spots, rows]
+
+
+def unpack(back, shape):
+    near = pl.BlockSpec(memory_space=pltpu.VMEM)
+    return pl.pallas_call(
+        unpack_kernel,
+        out_shape=jax.ShapeDtypeStruct(shape, back.dtype),
+        in_specs=[near],
+        out_specs=near,
+        name="unpack",
+    )(pltpu.with_memory_space_constraint(back, pltpu.VMEM))
 
 
 def local(queries, key_blocks, value_blocks, selected):
@@ -197,8 +234,7 @@
     pieces = exchange(sent.reshape(pair_size, width * piece, HD), PAIR)
     pieces = pieces.reshape(half_blocks, 2, width, piece, HD)
     done = attend(arrived, pieces, row_count, heads * row_count)
-    back = exchange(done, CTX).reshape(groups, half_blocks, heads, row_count, HD)
-    return back.transpose(1, 3, 0, 2, 4).reshape(queries.shape)
+    return unpack(exchange(done, CTX), queries.shape)
 
 
 def solution(mesh):

time: 144 us -> 144 us (level)
  Pallas kernels: 12.7 us -> 14.3 us
    pallas_call x1 -> x2, Pallas kernels: 6.77 us -> 9.22 us  [the longest x1 8.19 us: attend(): pl.pallas_call(functools.partial(attend_kernel, row_count, parts), out_sh...]
where the time goes in v5:
time: 144 us
  waiting for transfers between devices  62.7 us (44%)
  blocking collectives  50.2 us (35%)
  starting transfers between devices  15.4 us (11%)
  Pallas kernels  14.3 us (10%)
    all_to_all x1, waiting for transfers between devices, exchange(): return lax.all_to_all(value, axes, split_axis=0, concat_axis=0, tiled=True)  62.7 us
    all_to_all x2, blocking collectives, exchange(): return lax.all_to_all(value, axes, split_axis=0, concat_axis=0, tiled=True)  50.2 us
    all_to_all x1, starting transfers between devices, exchange(): return lax.all_to_all(value, axes, split_axis=0, concat_axis=0, tiled=True)  15.4 us
    pallas_call x1, Pallas kernels, attend(): pl.pallas_call(functools.partial(attend_kernel, row_count, parts), out_sh...  8.19 us
    pallas_call x1, Pallas kernels, pack(): pl.pallas_call(pack_kernel, out_shape=whole, in_specs=[pl.BlockSpec(memor...  3.02 us
  transfers between devices with their start and end apart: 1, of which 1 were waited for; matrix products, arithmetic and copies ran while one was open for 1% of the time, Pallas kernels for 0%

profile of v5, /device:TPU:2, one launch (start us, length us, event | category | flops | bytes accessed | tf_op | source)
XLA Modules:
  0.0 143.6 jit_solution(6478542019641453013)
XLA Ops:
  0.0 3.0 %pack.1 = bf16[128,80,128]{2,1,0:T(8,128)(2,1)} custom-call(s32[1]{0:T(128)} %bitcast.core_ref, bf16[32,4,2048]{2,1,0:T(4,128)(2,1)} %q_ref.1, bf16[4,32,16,512]{3,2,1,0:T(8,128)(2,1)} %bitcast.13, bf16[4,32,16,512]{3,2,1,0:T(8,128)(2,1)} %bitcast.14), custom_call_target="tpu_custom_call" | custom-call | tf_op jit(solution)/shard_map/pack/pallas_call | solution.py:70
  3.0 0.0 copy-start
  3.0 15.4 %all-to-all-start = ((bf16[128,80,128]{2,1,0:T(8,128)(2,1)}), bf16[128,80,128]{2,1,0:T(8,128)(2,1)S(1)}, u32[]{:S(2)}, u32[]{:S(2)}) async-start(bf16[128,80,128]{2,1,0:T(8,128)(2,1)} %pack.1), calls=%async_computation | async-start | bytes 5242880 | tf_op jit(solution)/shard_map/all_to_all | solution.py:17
  18.5 0.0 copy-done
  18.5 0.1 concatenate.6
  18.6 0.1 copy.8
  18.7 0.1 reshape.40
  18.8 0.6 fusion.index_ref
  19.4 62.7 %all-to-all-done.q_ref = bf16[128,80,128]{2,1,0:T(8,128)(2,1)S(1)} async-done(((bf16[128,80,128]{2,1,0:T(8,128)(2,1)}), bf16[128,80,128]{2,1,0:T(8,128)(2,1)S(1)}, u32[]{:S(2)}, u32[]{:S(2)}) %all-to-all-start) | async-done | bytes 2621472 | tf_op jit(solution)/shard_map/all_to_all | solution.py:17
  82.1 2.1 %pick.1 = bf16[256,16,128]{2,1,0:T(8,128)(2,1)} custom-call(s32[256]{0:T(256)} %fusion.index_ref, bf16[640,16,128]{2,1,0:T(8,128)(2,1)S(1)} %bitcast.10), custom_call_target="tpu_custom_call" | custom-call | tf_op jit(solution)/shard_map/pick/pallas_call | solution.py:103
  84.2 22.3 %all_to_all.15 = bf16[64,64,128]{2,1,0:T(8,128)(2,1)S(1)} all-to-all(bf16[64,64,128]{2,1,0:T(8,128)(2,1)} %bitcast.12), channel_id=1, replica_groups=mesh['zp'=4,'zl'=2,'x'=4,'y'=4,'c'=2] {'zl','x','y','c'}, dimensions={0} | all-to-all | bytes 2097152 | tf_op jit(solution)/shard_map/all_to_all | solution.py:17
  106.5 8.2 %attend.1 = bf16[128,16,128]{2,1,0:T(8,128)(2,1)S(1)} custom-call(bf16[128,80,128]{2,1,0:T(8,128)(2,1)S(1)} %all-to-all-done.q_ref, bf16[32,2,4,16,128]{4,3,2,1,0:T(8,128)(2,1)S(1)} %bitcast.11), custom_call_target="tpu_custom_call" | custom-call | tf_op jit(solution)/shard_map/attend/pallas_call | solution.py:173
  114.7 27.9 %all_to_all.16.back_ref = bf16[128,16,128]{2,1,0:T(8,128)(2,1)S(1)} all-to-all(bf16[128,16,128]{2,1,0:T(8,128)(2,1)S(1)} %attend.1), channel_id=1, replica_groups=mesh['zp'=4,'zl'=2,'x'=4,'y'=4,'c'=2] {'zp','zl','x','y'}, dimensions={0} | all-to-all | bytes 1048576 | tf_op jit(solution)/shard_map/all_to_all | solution.py:17
  142.6 1.0 unpack.1
  (3 shorter events, 0.0 us)
Async XLA Ops:
  3.0 15.5 %copy-start = (s32[64,3]{0,1:T(4,128)S(1)}, s32[64,3]{0,1:T(4,128)}, u32[]{:S(2)}) copy-start(s32[64,3]{0,1:T(4,128)} %param.7) | copy-start | bytes 2308
  3.0 79.0 %all-to-all-start = ((bf16[128,80,128]{2,1,0:T(8,128)(2,1)}), bf16[128,80,128]{2,1,0:T(8,128)(2,1)S(1)}, u32[]{:S(2)}, u32[]{:S(2)}) async-start(bf16[128,80,128]{2,1,0:T(8,128)(2,1)} %pack.1), calls=%async_computation | async-start | bytes 5242880 | tf_op jit(solution)/shard_map/all_to_all | solution.py:17

commit v6 on v5

--- a/solution.py
+++ b/solution.py
@@ -108,11 +108,12 @@
             pl.BlockSpec(memory_space=pltpu.VMEM),
         ],
         out_specs=pl.BlockSpec(memory_space=pltpu.VMEM),
+        compiler_params=pltpu.CompilerParams(vmem_limit_bytes=32 * 2**20),
         name="pick",
     )(index, table)
 
 
-def attend_kernel(row_count, parts, q_ref, kv_ref, out_ref, keys, values, ready, sems):
+def attend_kernel(row_count, parts, q_ref, kv_ref, out_ref, keys, values):
     spots, _, width, piece, _ = kv_ref.shape
     own_keys = spots * piece
     ctx_size, rows_each, _ = out_ref.shape
@@ -148,20 +149,13 @@
             weights = jnp.exp2((score - best) * factor).astype(jnp.bfloat16)
             mixed += jnp.dot(weights, values[pl.ds(*span)], preferred_element_type=jnp.float32)
         result = mixed[:, :HD] / mixed[:, HD:]
-        ready[held] = result.astype(out_ref.dtype).reshape(holders, rows_each, HD)
-        leave(part).start()
+        out_ref[held] = result.astype(out_ref.dtype).reshape(holders, rows_each, HD)
         yield
-
-    def leave(part):
-        held = pl.ds(part * holders, holders)
-        return pltpu.make_async_copy(ready.at[held], out_ref.at[held], sems.at[part])
 
     running = [steps(part) for part in range(parts)]
     for _ in range(3):
         for one in running:
             next(one)
-    for part in range(parts):
-        leave(part).wait()
 
 
 def attend(arrived, pieces, row_count, rows_each):
@@ -174,12 +168,10 @@
         functools.partial(attend_kernel, row_count, parts),
         out_shape=whole,
         in_specs=[near, near],
-        out_specs=pl.BlockSpec(memory_space=pl.ANY),
+        out_specs=near,
         scratch_shapes=[
             pltpu.VMEM((width * spots * piece, HD), jnp.bfloat16),
             pltpu.VMEM((width * spots * piece, 2 * HD), jnp.bfloat16),
-            pltpu.VMEM(whole.shape, whole.dtype),
-            pltpu.SemaphoreType.DMA((parts,)),
         ],
         compiler_params=pltpu.CompilerParams(vmem_limit_bytes=48 * 2**20),
         name="attend",

time: 144 us -> 139 us (0.965)
  Pallas kernels: 14.3 us -> 9.62 us
    pallas_call x1, Pallas kernels: 8.19 us -> 4.59 us  [attend(): pl.pallas_call(functools.partial(attend_kernel, row_count, parts), out_sh...]
  transfers between devices with their start and end apart: 1 -> 1, of which waited for: 1 -> 1; matrix products, arithmetic and copies ran while one was open for 1% -> 0% of each run, Pallas kernels for 0% -> 0%
where the time goes in v6:
time: 139 us
  waiting for transfers between devices  63.2 us (45%)
  blocking collectives  50 us (36%)
  starting transfers between devices  15.4 us (11%)
  Pallas kernels  9.62 us (7%)
    all_to_all x1, waiting for transfers between devices, exchange(): return lax.all_to_all(value, axes, split_axis=0, concat_axis=0, tiled=True)  63.2 us
    all_to_all x2, blocking collectives, exchange(): return lax.all_to_all(value, axes, split_axis=0, concat_axis=0, tiled=True)  50 us
    all_to_all x1, starting transfers between devices, exchange(): return lax.all_to_all(value, axes, split_axis=0, concat_axis=0, tiled=True)  15.4 us
    pallas_call x1, Pallas kernels, attend(): pl.pallas_call(functools.partial(attend_kernel, row_count, parts), out_sh...  4.59 us
    pallas_call x1, Pallas kernels, pack(): pl.pallas_call(pack_kernel, out_shape=whole, in_specs=[pl.BlockSpec(memor...  3.02 us
  transfers between devices with their start and end apart: 1, of which 1 were waited for; matrix products, arithmetic and copies ran while one was open for 0% of the time, Pallas kernels for 0%

profile of v6, /device:TPU:2, one launch (start us, length us, event | category | flops | bytes accessed | tf_op | source)
XLA Modules:
  0.0 138.7 jit_solution(10978249334919094633)
XLA Ops:
  0.0 3.0 %pack.1 = bf16[128,80,128]{2,1,0:T(8,128)(2,1)} custom-call(s32[1]{0:T(128)} %bitcast.core_ref, bf16[32,4,2048]{2,1,0:T(4,128)(2,1)} %q_ref.1, bf16[4,32,16,512]{3,2,1,0:T(8,128)(2,1)} %bitcast.13, bf16[4,32,16,512]{3,2,1,0:T(8,128)(2,1)} %bitcast.14), custom_call_target="tpu_custom_call" | custom-call | tf_op jit(solution)/shard_map/pack/pallas_call | solution.py:70
  3.0 0.0 copy-start
  3.0 15.4 %all-to-all-start = ((bf16[128,80,128]{2,1,0:T(8,128)(2,1)}), bf16[128,80,128]{2,1,0:T(8,128)(2,1)S(1)}, u32[]{:S(2)}, u32[]{:S(2)}) async-start(bf16[128,80,128]{2,1,0:T(8,128)(2,1)} %pack.1), calls=%async_computation | async-start | bytes 5242880 | tf_op jit(solution)/shard_map/all_to_all | solution.py:17
  18.5 0.0 copy-done
  18.5 0.1 concatenate.6
  18.6 0.1 copy.8
  18.7 0.1 reshape.40
  18.8 63.2 %all-to-all-done.q_ref = bf16[128,80,128]{2,1,0:T(8,128)(2,1)S(1)} async-done(((bf16[128,80,128]{2,1,0:T(8,128)(2,1)}), bf16[128,80,128]{2,1,0:T(8,128)(2,1)S(1)}, u32[]{:S(2)}, u32[]{:S(2)}) %all-to-all-start) | async-done | bytes 2621472 | tf_op jit(solution)/shard_map/all_to_all | solution.py:17
  82.1 1.0 pick.1
  83.1 22.1 %all_to_all.15 = bf16[64,64,128]{2,1,0:T(8,128)(2,1)S(1)} all-to-all(bf16[64,64,128]{2,1,0:T(8,128)(2,1)S(1)} %bitcast.12), channel_id=1, replica_groups=mesh['zp'=4,'zl'=2,'x'=4,'y'=4,'c'=2] {'zl','x','y','c'}, dimensions={0} | all-to-all | bytes 2097152 | tf_op jit(solution)/shard_map/all_to_all | solution.py:17
  105.2 4.6 %attend.1 = bf16[128,16,128]{2,1,0:T(8,128)(2,1)S(1)} custom-call(bf16[128,80,128]{2,1,0:T(8,128)(2,1)S(1)} %all-to-all-done.q_ref, bf16[32,2,4,16,128]{4,3,2,1,0:T(8,128)(2,1)S(1)} %bitcast.11), custom_call_target="tpu_custom_call" | custom-call | tf_op jit(solution)/shard_map/attend/pallas_call | solution.py:167
  109.8 27.9 %all_to_all.16.back_ref = bf16[128,16,128]{2,1,0:T(8,128)(2,1)S(1)} all-to-all(bf16[128,16,128]{2,1,0:T(8,128)(2,1)S(1)} %attend.1), channel_id=1, replica_groups=mesh['zp'=4,'zl'=2,'x'=4,'y'=4,'c'=2] {'zp','zl','x','y'}, dimensions={0} | all-to-all | bytes 1048576 | tf_op jit(solution)/shard_map/all_to_all | solution.py:17
  137.7 1.0 unpack.1
  (4 shorter events, 0.0 us)
Async XLA Ops:
  3.0 15.5 %copy-start = (s32[64,3]{0,1:T(4,128)S(1)}, s32[64,3]{0,1:T(4,128)}, u32[]{:S(2)}) copy-start(s32[64,3]{0,1:T(4,128)} %param.7) | copy-start | bytes 2308
  3.0 79.0 %all-to-all-start = ((bf16[128,80,128]{2,1,0:T(8,128)(2,1)}), bf16[128,80,128]{2,1,0:T(8,128)(2,1)S(1)}, u32[]{:S(2)}, u32[]{:S(2)}) async-start(bf16[128,80,128]{2,1,0:T(8,128)(2,1)} %pack.1), calls=%async_computation | async-start | bytes 5242880 | tf_op jit(solution)/shard_map/all_to_all | solution.py:17

commit v7 on v6

--- a/solution.py
+++ b/solution.py
@@ -17,7 +17,9 @@
     return lax.all_to_all(value, axes, split_axis=0, concat_axis=0, tiled=True)
 
 
-def pack_kernel(core_ref, q_ref, k_ref, v_ref, out_ref, asked, held, q_sem, in_sems, out_sems):
+def pack_kernel(
+    core_ref, chosen_ref, q_ref, k_ref, v_ref, out_ref, place_ref, asked, q_sem, in_sems
+):
     kv_count, spots, piece, kv_width = k_ref.shape
     _, row_count, feat_width = q_ref.shape
     groups = kv_width // HD
@@ -26,13 +28,9 @@
     def fetch(ref, g, one):
         return pltpu.make_async_copy(
             ref.at[one, :, :, pl.ds(g * HD, HD)],
-            held.at[pl.ds(g * spots, spots), pl.ds(one * piece, piece)],
+            out_ref.at[pl.ds(g * spots, spots), pl.ds(one * piece, piece)],
             in_sems.at[g, one],
         )
-
-    def leave(g):
-        part = pl.ds(g * spots, spots)
-        return pltpu.make_async_copy(held.at[part], out_ref.at[part], out_sems.at[g])
 
     whole = pltpu.make_async_copy(q_ref, asked, q_sem)
     whole.start()
@@ -44,48 +42,65 @@
                 for one in range(kv_count):
                     fetch(ref, g, one).start()
 
+    topk, block_total = chosen_ref.shape
+    width = topk + 1
+    in_parcel = out_ref.shape[1] // piece
+    first_own = out_ref.shape[0] * kv_count - block_total
+
+    def note(spot, carry):
+        for half in range(2):
+            asker = half * spots + spot
+            named = [first_own + asker] + [chosen_ref[j, asker] for j in range(topk)]
+            for j, target in enumerate(named):
+                holder = lax.div(target, kv_count)
+                inner = target - holder * kv_count
+                place_ref[(spot * 2 + half) * width + j] = holder * in_parcel + inner
+        return carry
+
+    lax.fori_loop(0, spots, note, 0)
     whole.wait()
     for g in range(groups):
         for head in range(heads):
             rows = pl.ds(kv_count * piece + head * row_count, row_count)
             at = (g * heads + head) * HD
-            held[pl.ds(g * spots, spots), rows] = asked[:, :, at : at + HD]
+            out_ref[pl.ds(g * spots, spots), rows] = asked[:, :, at : at + HD]
     for g in range(groups):
         for one in range(kv_count):
             fetch(k_ref, g, one).wait()
-        leave(g).start()
-    for g in range(groups):
-        leave(g).wait()
-
-
-def pack(core, queries, key_blocks, value_blocks):
+
+
+def pack(core, selected, queries, key_blocks, value_blocks):
     kv_count, block, kv_width = key_blocks.shape
     groups = kv_width // HD
     half_blocks, row_count, feat_width = queries.shape
     piece = block // half_blocks
     tall = kv_count * piece + feat_width // kv_width * row_count
-    whole = jax.ShapeDtypeStruct((groups * half_blocks, tall, HD), queries.dtype)
     cut = (kv_count, half_blocks, piece, kv_width)
-    away = pl.BlockSpec(memory_space=pl.ANY)
+    scalars = pl.BlockSpec(memory_space=pltpu.SMEM)
+    away = pl.BlockSpec(memory_space=pltpu.HBM)
+    count = selected.shape[0] * (selected.shape[1] + 1)
     return pl.pallas_call(
         pack_kernel,
-        out_shape=whole,
-        in_specs=[
-            pl.BlockSpec(memory_space=pltpu.SMEM),
-            away,
-            away,
-            away,
-        ],
-        out_specs=away,
+        out_shape=(
+            jax.ShapeDtypeStruct((groups * half_blocks, tall, HD), queries.dtype),
+            jax.ShapeDtypeStruct((count,), jnp.int32),
+        ),
+        in_specs=[scalars, scalars, away, away, away],
+        out_specs=(pl.BlockSpec(memory_space=pltpu.VMEM), scalars),
         scratch_shapes=[
             pltpu.VMEM(queries.shape, queries.dtype),
-            pltpu.VMEM(whole.shape, whole.dtype),
             pltpu.SemaphoreType.DMA(()),
             pltpu.SemaphoreType.DMA((groups, kv_count)),
-            pltpu.SemaphoreType.DMA((groups,)),
         ],
+        compiler_params=pltpu.CompilerParams(vmem_limit_bytes=32 * 2**20),
         name="pack",
-    )(core[None], queries, key_blocks.reshape(cut), value_blocks.reshape(cut))
+    )(
+        core[None],
+        *(
+            pltpu.with_memory_space_constraint(array, pltpu.HBM)
+            for array in (selected.T, queries, key_blocks.reshape(cut), value_blocks.reshape(cut))
+        ),
+    )
 
 
 def pick_kernel(index_ref, table_ref, out_ref):
@@ -211,17 +226,10 @@
     ctx_size = lax.axis_size(CTX)
     pair_size = lax.axis_size(PAIR)
     piece = block // half_blocks
-    parcels = pack(core, queries, key_blocks, value_blocks)
+    width = selected.shape[1] + 1
+    parcels, place = pack(core, selected, queries, key_blocks, value_blocks)
     arrived = exchange(parcels, CTX)
-
-    block_total = selected.shape[0]
-    own_block = ctx_size * kv_count - block_total + jnp.arange(block_total, dtype=jnp.int32)
-    targets = jnp.concatenate([own_block[:, None], selected], axis=1)
-    width = targets.shape[1]
-    targets = targets.reshape(2, half_blocks, width).transpose(1, 0, 2).reshape(-1)
-    in_parcel = parcels.shape[1] // piece
-    place = targets // kv_count * in_parcel + targets % kv_count
-    table = arrived.reshape(ctx_size * in_parcel, piece, HD)
+    table = arrived.reshape(-1, piece, HD)
     sent = pick(place, pltpu.with_memory_space_constraint(table, pltpu.VMEM))
     pieces = exchange(sent.reshape(pair_size, width * piece, HD), PAIR)
     pieces = pieces.reshape(half_blocks, 2, width, piece, HD)

time: 139 us -> 139 us (level)
  blocking collectives: 50 us -> 129 us
  waiting for transfers between devices: 63.2 us -> 0 us
  starting transfers between devices: 15.4 us -> 0 us
    all_to_all x2 -> x3, blocking collectives: 50 us -> 129 us  [exchange(): return lax.all_to_all(value, axes, split_axis=0, concat_axis=0, tiled=True)]
    all_to_all x1 -> x0, waiting for transfers between devices: 63.2 us -> none  [exchange(): return lax.all_to_all(value, axes, split_axis=0, concat_axis=0, tiled=True)]
    all_to_all x1 -> x0, starting transfers between devices: 15.4 us -> none  [exchange(): return lax.all_to_all(value, axes, split_axis=0, concat_axis=0, tiled=True)]
  transfers between devices with their start and end apart: 1 -> 0, of which waited for: 1 -> 0; matrix products, arithmetic and copies ran while one was open for 0% -> 0% of each run, Pallas kernels for 0% -> 0%
where the time goes in v7:
time: 139 us
  blocking collectives  129 us (93%)
  Pallas kernels  9.78 us (7%)
    all_to_all x3, blocking collectives, exchange(): return lax.all_to_all(value, axes, split_axis=0, concat_axis=0, tiled=True)  129 us
    pallas_call x1, Pallas kernels, attend(): pl.pallas_call(functools.partial(attend_kernel, row_count, parts), out_sh...  4.59 us
    pallas_call x1, Pallas kernels, pack(): pl.pallas_call(pack_kernel, out_shape=(jax.ShapeDtypeStruct((groups * hal...  3.17 us

profile of v7, /device:TPU:2, one launch (start us, length us, event | category | flops | bytes accessed | tf_op | source)
XLA Modules:
  0.0 138.7 jit_solution(11874847607052480553)
XLA Ops:
  0.0 3.2 %pack.1 = (bf16[128,80,128]{2,1,0:T(8,128)(2,1)S(1)}, s32[256]{0:T(256)S(1)}) custom-call(s32[1]{0:T(128)} %bitcast.core_ref, s32[3,64]{1,0:T(4,128)} %bitcast.12, bf16[32,4,2048]{2,1,0:T(4,128)(2,1)} %q_ref.1, bf16[4,32,16,512]{3,2,1,0:T(8,128)(2,1)} %bitcast.10, bf16[4,32,16,512]{3,2,1,0:T(8,128)(2,1)} %bitcast.11), custom_call_target="tpu_custom_call" | custom-call | tf_op jit(solution)/shard_map/pack/pallas_call | solution.py:82
  3.2 78.8 %all_to_all.15.q_ref = bf16[128,80,128]{2,1,0:T(8,128)(2,1)S(1)} all-to-all(bf16[128,80,128]{2,1,0:T(8,128)(2,1)S(1)} %get-tuple-element.7), channel_id=1, replica_groups=mesh['zp'=4,'zl'=2,'x'=4,'y'=4,'c'=2] {'zp','zl','x','y'}, dimensions={0} | all-to-all | bytes 5242880 | tf_op jit(solution)/shard_map/all_to_all | solution.py:17
  82.0 1.0 pick.1
  83.0 22.1 %all_to_all.16 = bf16[64,64,128]{2,1,0:T(8,128)(2,1)S(1)} all-to-all(bf16[64,64,128]{2,1,0:T(8,128)(2,1)S(1)} %bitcast.9), channel_id=1, replica_groups=mesh['zp'=4,'zl'=2,'x'=4,'y'=4,'c'=2] {'zl','x','y','c'}, dimensions={0} | all-to-all | bytes 2097152 | tf_op jit(solution)/shard_map/all_to_all | solution.py:17
  105.1 4.6 %attend.1 = bf16[128,16,128]{2,1,0:T(8,128)(2,1)S(1)} custom-call(bf16[128,80,128]{2,1,0:T(8,128)(2,1)S(1)} %all_to_all.15.q_ref, bf16[32,2,4,16,128]{4,3,2,1,0:T(8,128)(2,1)S(1)} %bitcast.8), custom_call_target="tpu_custom_call" | custom-call | tf_op jit(solution)/shard_map/attend/pallas_call | solution.py:182
  109.7 27.9 %all_to_all.17.back_ref = bf16[128,16,128]{2,1,0:T(8,128)(2,1)S(1)} all-to-all(bf16[128,16,128]{2,1,0:T(8,128)(2,1)S(1)} %attend.1), channel_id=1, replica_groups=mesh['zp'=4,'zl'=2,'x'=4,'y'=4,'c'=2] {'zp','zl','x','y'}, dimensions={0} | all-to-all | bytes 1048576 | tf_op jit(solution)/shard_map/all_to_all | solution.py:17
  137.6 1.0 unpack.1

commit v8 on v7

--- a/solution.py
+++ b/solution.py
@@ -10,6 +10,7 @@
 
 HD = 128
 CTX = ("zp", "zl", "x", "y")
+SPREAD = ("zl", "x", "y", "zp")
 PAIR = ("zl", "x", "y", "c")
 
 
@@ -28,7 +29,7 @@
     def fetch(ref, g, one):
         return pltpu.make_async_copy(
             ref.at[one, :, :, pl.ds(g * HD, HD)],
-            out_ref.at[pl.ds(g * spots, spots), pl.ds(one * piece, piece)],
+            out_ref.at[:, g, pl.ds(one * piece, piece)],
             in_sems.at[g, one],
         )
 
@@ -44,8 +45,8 @@
 
     topk, block_total = chosen_ref.shape
     width = topk + 1
-    in_parcel = out_ref.shape[1] // piece
-    first_own = out_ref.shape[0] * kv_count - block_total
+    in_parcel = out_ref.shape[2] // piece
+    first_own = spots * groups * kv_count - block_total
 
     def note(spot, carry):
         for half in range(2):
@@ -54,7 +55,9 @@
             for j, target in enumerate(named):
                 holder = lax.div(target, kv_count)
                 inner = target - holder * kv_count
-                place_ref[(spot * 2 + half) * width + j] = holder * in_parcel + inner
+                pair = lax.div(holder, spots)
+                came = (holder - pair * spots) * groups + pair
+                place_ref[(spot * 2 + half) * width + j] = came * in_parcel + inner
         return carry
 
     lax.fori_loop(0, spots, note, 0)
@@ -63,7 +66,7 @@
         for head in range(heads):
             rows = pl.ds(kv_count * piece + head * row_count, row_count)
             at = (g * heads + head) * HD
-            out_ref[pl.ds(g * spots, spots), rows] = asked[:, :, at : at + HD]
+            out_ref[:, g, rows] = asked[:, :, at : at + HD]
     for g in range(groups):
         for one in range(kv_count):
             fetch(k_ref, g, one).wait()
@@ -82,7 +85,7 @@
     return pl.pallas_call(
         pack_kernel,
         out_shape=(
-            jax.ShapeDtypeStruct((groups * half_blocks, tall, HD), queries.dtype),
+            jax.ShapeDtypeStruct((half_blocks, groups, tall, HD), queries.dtype),
             jax.ShapeDtypeStruct((count,), jnp.int32),
         ),
         in_specs=[scalars, scalars, away, away, away],
@@ -131,9 +134,10 @@
 def attend_kernel(row_count, parts, q_ref, kv_ref, out_ref, keys, values):
     spots, _, width, piece, _ = kv_ref.shape
     own_keys = spots * piece
-    ctx_size, rows_each, _ = out_ref.shape
-    lead = q_ref.shape[1] - rows_each
-    holders = ctx_size // parts
+    _, groups, rows_each, _ = out_ref.shape
+    lead = q_ref.shape[2] - rows_each
+    holders = spots * groups // parts
+    per_group = spots // holders
     rows = holders * rows_each
     factor = math.log2(math.e) / math.sqrt(HD)
     nt = (((1,), (1,)), ((), ()))
@@ -144,8 +148,9 @@
     values[:, HD:] = jnp.ones((width * own_keys, HD), jnp.bfloat16)
 
     def steps(part):
-        held = pl.ds(part * holders, holders)
-        asked = q_ref[held, lead:].reshape(rows, HD)
+        held = pl.ds(part % per_group * holders, holders)
+        pair = part // per_group
+        asked = q_ref[held, pair, lead:].reshape(rows, HD)
         seen = min(own_keys, -(-(part + 1) * holders * row_count // 128) * 128)
         spans = [(0, seen)] + [(j * own_keys, own_keys) for j in range(1, width)]
         scores = [
@@ -164,7 +169,7 @@
             weights = jnp.exp2((score - best) * factor).astype(jnp.bfloat16)
             mixed += jnp.dot(weights, values[pl.ds(*span)], preferred_element_type=jnp.float32)
         result = mixed[:, :HD] / mixed[:, HD:]
-        out_ref[held] = result.astype(out_ref.dtype).reshape(holders, rows_each, HD)
+        out_ref[held, pair] = result.astype(out_ref.dtype).reshape(holders, rows_each, HD)
         yield
 
     running = [steps(part) for part in range(parts)]
@@ -174,10 +179,9 @@
 
 
 def attend(arrived, pieces, row_count, rows_each):
-    ctx_size = arrived.shape[0]
     spots, _, width, piece, _ = pieces.shape
     parts = 8
-    whole = jax.ShapeDtypeStruct((ctx_size, rows_each, HD), jnp.bfloat16)
+    whole = jax.ShapeDtypeStruct(arrived.shape[:2] + (rows_each, HD), jnp.bfloat16)
     near = pl.BlockSpec(memory_space=pltpu.VMEM)
     return pl.pallas_call(
         functools.partial(attend_kernel, row_count, parts),
@@ -197,13 +201,14 @@
 
 
 def unpack_kernel(back_ref, out_ref):
-    spots, row_count, feat_width = out_ref.shape
-    heads = back_ref.shape[1] // row_count
-    for g in range(back_ref.shape[0] // spots):
+    row_count = out_ref.shape[1]
+    _, groups, rows_each, _ = back_ref.shape
+    heads = rows_each // row_count
+    for g in range(groups):
         for head in range(heads):
             at = (g * heads + head) * HD
             rows = pl.ds(head * row_count, row_count)
-            out_ref[:, :, at : at + HD] = back_ref[g * spots : (g + 1) * spots, rows]
+            out_ref[:, :, at : at + HD] = back_ref[:, g, rows]
 
 
 def unpack(back, shape):
@@ -221,20 +226,20 @@
     core = lax.axis_index("c")
     half_blocks, row_count, feat_width = queries.shape
     kv_count, block, kv_width = key_blocks.shape
-    groups = kv_width // HD
     heads = feat_width // kv_width
-    ctx_size = lax.axis_size(CTX)
     pair_size = lax.axis_size(PAIR)
     piece = block // half_blocks
     width = selected.shape[1] + 1
     parcels, place = pack(core, selected, queries, key_blocks, value_blocks)
-    arrived = exchange(parcels, CTX)
+    laid = parcels.shape
+    arrived = exchange(parcels.reshape((-1,) + laid[2:]), SPREAD)
     table = arrived.reshape(-1, piece, HD)
     sent = pick(place, pltpu.with_memory_space_constraint(table, pltpu.VMEM))
     pieces = exchange(sent.reshape(pair_size, width * piece, HD), PAIR)
     pieces = pieces.reshape(half_blocks, 2, width, piece, HD)
-    done = attend(arrived, pieces, row_count, heads * row_count)
-    return unpack(exchange(done, CTX), queries.shape)
+    done = attend(arrived.reshape(laid), pieces, row_count, heads * row_count)
+    back = exchange(done.reshape((-1,) + done.shape[2:]), SPREAD)
+    return unpack(back.reshape(done.shape), queries.shape)
 
 
 def solution(mesh):

time: 139 us -> 139 us (level); the launches traced: 139 us -> 137 us
  blocking collectives: 129 us -> 127 us
    all_to_all x3, blocking collectives: 129 us -> 127 us  [exchange(): return lax.all_to_all(value, axes, split_axis=0, concat_axis=0, tiled=True)]
where the time goes in v8:
time: 139 us; the launch traced here: 137 us
  blocking collectives  127 us (91%)
  Pallas kernels  10.2 us (7%)
    all_to_all x3, blocking collectives, exchange(): return lax.all_to_all(value, axes, split_axis=0, concat_axis=0, tiled=True)  127 us
    pallas_call x1, Pallas kernels, attend(): pl.pallas_call(functools.partial(attend_kernel, row_count, parts), out_sh...  4.59 us
    pallas_call x1, Pallas kernels, pack(): pl.pallas_call(pack_kernel, out_shape=(jax.ShapeDtypeStruct((half_blocks,...  3.65 us

profile of v8, /device:TPU:2, one launch (start us, length us, event | category | flops | bytes accessed | tf_op | source)
XLA Modules:
  0.0 137.1 jit_solution(3289284052759611820)
XLA Ops:
  0.0 3.6 %pack.1 = (bf16[32,4,80,128]{3,2,1,0:T(8,128)(2,1)S(1)}, s32[256]{0:T(256)S(1)}) custom-call(s32[1]{0:T(128)} %bitcast.core_ref, s32[3,64]{1,0:T(4,128)} %bitcast.20, bf16[32,4,2048]{2,1,0:T(4,128)(2,1)} %q_ref.1, bf16[4,32,16,512]{3,2,1,0:T(8,128)(2,1)} %bitcast.18, bf16[4,32,16,512]{3,2,1,0:T(8,128)(2,1)} %bitcast.19), custom_call_target="tpu_custom_call" | custom-call | tf_op jit(solution)/shard_map/pack/pallas_call | solution.py:85
  3.7 77.7 %all_to_all.15 = bf16[128,80,128]{2,1,0:T(8,128)(2,1)S(1)} all-to-all(bf16[128,80,128]{2,1,0:T(8,128)(2,1)S(1)} %bitcast.15), channel_id=1, replica_groups=mesh['zp'=4,'zl'=2,'x'=4,'y'=4,'c'=2] {'zl','x','y','zp'}, dimensions={0} | all-to-all | bytes 5242880 | tf_op jit(solution)/shard_map/all_to_all | solution.py:18
  81.3 1.0 pick.1
  82.3 24.2 %all_to_all.16 = bf16[64,64,128]{2,1,0:T(8,128)(2,1)S(1)} all-to-all(bf16[64,64,128]{2,1,0:T(8,128)(2,1)S(1)} %bitcast.14), channel_id=1, replica_groups=mesh['zp'=4,'zl'=2,'x'=4,'y'=4,'c'=2] {'zl','x','y','c'}, dimensions={0} | all-to-all | bytes 2097152 | tf_op jit(solution)/shard_map/all_to_all | solution.py:18
  106.5 4.6 %attend.1 = bf16[32,4,16,128]{3,2,1,0:T(8,128)(2,1)S(1)} custom-call(bf16[32,4,80,128]{3,2,1,0:T(8,128)(2,1)S(1)} %bitcast.12, bf16[32,2,4,16,128]{4,3,2,1,0:T(8,128)(2,1)S(1)} %bitcast.13), custom_call_target="tpu_custom_call" | custom-call | tf_op jit(solution)/shard_map/attend/pallas_call | solution.py:186
  111.1 25.0 %all_to_all.17 = bf16[128,16,128]{2,1,0:T(8,128)(2,1)S(1)} all-to-all(bf16[128,16,128]{2,1,0:T(8,128)(2,1)S(1)} %bitcast.17), channel_id=1, replica_groups=mesh['zp'=4,'zl'=2,'x'=4,'y'=4,'c'=2] {'zl','x','y','zp'}, dimensions={0} | all-to-all | bytes 1048576 | tf_op jit(solution)/shard_map/all_to_all | solution.py:18
  136.1 1.0 unpack.1

commit v9 on v8

--- a/solution.py
+++ b/solution.py
@@ -48,15 +48,18 @@
     in_parcel = out_ref.shape[2] // piece
     first_own = spots * groups * kv_count - block_total
 
+    assert kv_count & (kv_count - 1) == 0 and spots & (spots - 1) == 0
+    kv_bits, spot_bits = kv_count.bit_length() - 1, spots.bit_length() - 1
+
     def note(spot, carry):
         for half in range(2):
             asker = half * spots + spot
             named = [first_own + asker] + [chosen_ref[j, asker] for j in range(topk)]
             for j, target in enumerate(named):
-                holder = lax.div(target, kv_count)
-                inner = target - holder * kv_count
-                pair = lax.div(holder, spots)
-                came = (holder - pair * spots) * groups + pair
+                holder = lax.shift_right_logical(target, kv_bits)
+                inner = lax.bitwise_and(target, kv_count - 1)
+                pair = lax.shift_right_logical(holder, spot_bits)
+                came = lax.bitwise_and(holder, spots - 1) * groups + pair
                 place_ref[(spot * 2 + half) * width + j] = came * in_parcel + inner
         return carry
 

time: 139 us -> 138 us (level)
  no operation moved by 1% of the time
where the time goes in v9:
time: 138 us; the launch traced here: 137 us
  blocking collectives  127 us (92%)
  Pallas kernels  9.77 us (7%)
    all_to_all x3, blocking collectives, exchange(): return lax.all_to_all(value, axes, split_axis=0, concat_axis=0, tiled=True)  127 us
    pallas_call x1, Pallas kernels, attend(): pl.pallas_call(functools.partial(attend_kernel, row_count, parts), out_sh...  4.59 us
    pallas_call x1, Pallas kernels, pack(): pl.pallas_call(pack_kernel, out_shape=(jax.ShapeDtypeStruct((half_blocks,...  3.17 us

profile of v9, /device:TPU:2, one launch (start us, length us, event | category | flops | bytes accessed | tf_op | source)
XLA Modules:
  0.0 136.7 jit_solution(2897050566600387515)
XLA Ops:
  0.0 3.2 %pack.1 = (bf16[32,4,80,128]{3,2,1,0:T(8,128)(2,1)S(1)}, s32[256]{0:T(256)S(1)}) custom-call(s32[1]{0:T(128)} %bitcast.core_ref, s32[3,64]{1,0:T(4,128)} %bitcast.20, bf16[32,4,2048]{2,1,0:T(4,128)(2,1)} %q_ref.1, bf16[4,32,16,512]{3,2,1,0:T(8,128)(2,1)} %bitcast.18, bf16[4,32,16,512]{3,2,1,0:T(8,128)(2,1)} %bitcast.19), custom_call_target="tpu_custom_call" | custom-call | tf_op jit(solution)/shard_map/pack/pallas_call | solution.py:88
  3.2 77.7 %all_to_all.15 = bf16[128,80,128]{2,1,0:T(8,128)(2,1)S(1)} all-to-all(bf16[128,80,128]{2,1,0:T(8,128)(2,1)S(1)} %bitcast.15), channel_id=1, replica_groups=mesh['zp'=4,'zl'=2,'x'=4,'y'=4,'c'=2] {'zl','x','y','zp'}, dimensions={0} | all-to-all | bytes 5242880 | tf_op jit(solution)/shard_map/all_to_all | solution.py:18
  80.8 1.0 pick.1
  81.8 24.2 %all_to_all.16 = bf16[64,64,128]{2,1,0:T(8,128)(2,1)S(1)} all-to-all(bf16[64,64,128]{2,1,0:T(8,128)(2,1)S(1)} %bitcast.14), channel_id=1, replica_groups=mesh['zp'=4,'zl'=2,'x'=4,'y'=4,'c'=2] {'zl','x','y','c'}, dimensions={0} | all-to-all | bytes 2097152 | tf_op jit(solution)/shard_map/all_to_all | solution.py:18
  106.0 4.6 %attend.1 = bf16[32,4,16,128]{3,2,1,0:T(8,128)(2,1)S(1)} custom-call(bf16[32,4,80,128]{3,2,1,0:T(8,128)(2,1)S(1)} %bitcast.12, bf16[32,2,4,16,128]{4,3,2,1,0:T(8,128)(2,1)S(1)} %bitcast.13), custom_call_target="tpu_custom_call" | custom-call | tf_op jit(solution)/shard_map/attend/pallas_call | solution.py:189
  110.6 25.0 %all_to_all.17 = bf16[128,16,128]{2,1,0:T(8,128)(2,1)S(1)} all-to-all(bf16[128,16,128]{2,1,0:T(8,128)(2,1)S(1)} %bitcast.17), channel_id=1, replica_groups=mesh['zp'=4,'zl'=2,'x'=4,'y'=4,'c'=2] {'zl','x','y','zp'}, dimensions={0} | all-to-all | bytes 1048576 | tf_op jit(solution)/shard_map/all_to_all | solution.py:18
  135.6 1.0 unpack.1

commit v10 on v9

--- a/solution.py
+++ b/solution.py
@@ -34,7 +34,6 @@
         )
 
     whole = pltpu.make_async_copy(q_ref, asked, q_sem)
-    whole.start()
     for core, ref in enumerate((k_ref, v_ref)):
 
         @pl.when(core_ref[0] == core)
@@ -43,6 +42,7 @@
                 for one in range(kv_count):
                     fetch(ref, g, one).start()
 
+    whole.start()
     topk, block_total = chosen_ref.shape
     width = topk + 1
     in_parcel = out_ref.shape[2] // piece
@@ -111,12 +111,12 @@
 
 def pick_kernel(index_ref, table_ref, out_ref):
     def body(step, carry):
-        for inner in range(8):
-            place = step * 8 + inner
+        for inner in range(32):
+            place = step * 32 + inner
             out_ref[place] = table_ref[index_ref[place]]
         return carry
 
-    lax.fori_loop(0, out_ref.shape[0] // 8, body, 0)
+    lax.fori_loop(0, out_ref.shape[0] // 32, body, 0)
 
 
 def pick(index, table):

time: 138 us -> 138 us (level)
  no operation moved by 1% of the time
where the time goes in v10:
time: 138 us; the launch traced here: 137 us
  blocking collectives  127 us (92%)
  Pallas kernels  10.1 us (7%)
    all_to_all x3, blocking collectives, exchange(): return lax.all_to_all(value, axes, split_axis=0, concat_axis=0, tiled=True)  127 us
    pallas_call x1, Pallas kernels, attend(): pl.pallas_call(functools.partial(attend_kernel, row_count, parts), out_sh...  4.59 us
    pallas_call x1, Pallas kernels, pack(): pl.pallas_call(pack_kernel, out_shape=(jax.ShapeDtypeStruct((half_blocks,...  3.61 us

profile of v10, /device:TPU:2, one launch (start us, length us, event | category | flops | bytes accessed | tf_op | source)
XLA Modules:
  0.0 137.0 jit_solution(17457211822517049951)
XLA Ops:
  0.0 3.6 %pack.1 = (bf16[32,4,80,128]{3,2,1,0:T(8,128)(2,1)S(1)}, s32[256]{0:T(256)S(1)}) custom-call(s32[1]{0:T(128)} %bitcast.core_ref, s32[3,64]{1,0:T(4,128)} %bitcast.20, bf16[32,4,2048]{2,1,0:T(4,128)(2,1)} %q_ref.1, bf16[4,32,16,512]{3,2,1,0:T(8,128)(2,1)} %bitcast.18, bf16[4,32,16,512]{3,2,1,0:T(8,128)(2,1)} %bitcast.19), custom_call_target="tpu_custom_call" | custom-call | tf_op jit(solution)/shard_map/pack/pallas_call | solution.py:88
  3.6 77.7 %all_to_all.15 = bf16[128,80,128]{2,1,0:T(8,128)(2,1)S(1)} all-to-all(bf16[128,80,128]{2,1,0:T(8,128)(2,1)S(1)} %bitcast.15), channel_id=1, replica_groups=mesh['zp'=4,'zl'=2,'x'=4,'y'=4,'c'=2] {'zl','x','y','zp'}, dimensions={0} | all-to-all | bytes 5242880 | tf_op jit(solution)/shard_map/all_to_all | solution.py:18
  81.3 0.8 pick.1
  82.1 24.2 %all_to_all.16 = bf16[64,64,128]{2,1,0:T(8,128)(2,1)S(1)} all-to-all(bf16[64,64,128]{2,1,0:T(8,128)(2,1)S(1)} %bitcast.14), channel_id=1, replica_groups=mesh['zp'=4,'zl'=2,'x'=4,'y'=4,'c'=2] {'zl','x','y','c'}, dimensions={0} | all-to-all | bytes 2097152 | tf_op jit(solution)/shard_map/all_to_all | solution.py:18
  106.3 4.6 %attend.1 = bf16[32,4,16,128]{3,2,1,0:T(8,128)(2,1)S(1)} custom-call(bf16[32,4,80,128]{3,2,1,0:T(8,128)(2,1)S(1)} %bitcast.12, bf16[32,2,4,16,128]{4,3,2,1,0:T(8,128)(2,1)S(1)} %bitcast.13), custom_call_target="tpu_custom_call" | custom-call | tf_op jit(solution)/shard_map/attend/pallas_call | solution.py:189
  110.9 25.0 %all_to_all.17 = bf16[128,16,128]{2,1,0:T(8,128)(2,1)S(1)} all-to-all(bf16[128,16,128]{2,1,0:T(8,128)(2,1)S(1)} %bitcast.17), channel_id=1, replica_groups=mesh['zp'=4,'zl'=2,'x'=4,'y'=4,'c'=2] {'zl','x','y','zp'}, dimensions={0} | all-to-all | bytes 1048576 | tf_op jit(solution)/shard_map/all_to_all | solution.py:18
  135.9 1.0 unpack.1
